TPU v7x, 128 devices: a whole 4x4x4 slice. The times are simulated.
128 devices in a mesh: dp: 4 (over z_lo, core), tensor: 32 (over x, z_hi, y).
Axes of the slice: x: 4, y: 4, z: 4 (z_hi: 2, z_lo: 2; z = z_hi * 2 + z_lo), core: 2. Of those that a mesh axis runs over, the one named last changes fastest.
Arguments:
- hidden: bfloat16 [2048, 4096], P('dp'), may hold values from -6 to 6
- segment_ids: int32 [2048], P('dp'), may hold values from 0 to 31, as said below
- first_gain: float32 [4096], replicated, may hold values from 0.1 to 1.9
- second_gain: float32 [4096], replicated, may hold values from 0.1 to 1.9
- qkv_master: float32 [4096, 3, 4096], P(('dp', 'tensor'))
- out_master: float32 [4096, 4096], P(None, ('dp', 'tensor')), may hold values from -0.09375 to 0.09375
- up_master: float32 [4096, 16384], P(('dp', 'tensor')), may hold values from -0.09375 to 0.09375
- down_master: float32 [16384, 4096], P(None, ('dp', 'tensor')), may hold values from -0.046875 to 0.046875
Outputs:
- new_hidden: bfloat16 [2048, 4096], P(('dp', 'tensor'))
- key_cache: bfloat16 [2048, 4096], P('dp', 'tensor')
- value_cache: bfloat16 [2048, 4096], P('dp', 'tensor')
- qkv_block: bfloat16 [4096, 3, 4096], P(None, None, 'tensor')
- out_block: bfloat16 [4096, 4096], P('tensor')
- up_block: bfloat16 [4096, 16384], P(None, 'tensor')
- down_block: bfloat16 [16384, 4096], P('tensor')
Inputs may be any that keep to these rules, and one draw needn't show every extreme that they name: `segment_ids`: never falls along the tokens; group g holds exactly the 8 prompts 8 g to 8 g + 7, each of 1 to 505 tokens, and in some group one prompt has exactly 505 tokens.
All inputs are finite; a program needn't handle non-finite values.
Results may differ from a plain program's by a relative error of at most 0.029.
Values may be sent and summed in bfloat16 or wider, within the bound.
A program may use at most 128 MiB of HBM per device.

v0:
```python
import math

import jax
import jax.numpy as jnp
from jax import lax
from jax.sharding import PartitionSpec as P

D = 4096
HD = 128


EPSILON = 1e-05


def layer_norm(values, gain):
    values = values.astype(jnp.float32)
    center = values - jnp.mean(values, axis=-1, keepdims=True)
    spread = jnp.mean(center * center, axis=-1, keepdims=True)
    return center * lax.rsqrt(spread + EPSILON) * gain


def reorder(joined, groups, lanes):
    shape = joined.shape
    block = shape[0] // (groups * lanes)
    split_up = joined.reshape((lanes, groups, block) + shape[1:])
    return jnp.swapaxes(split_up, 0, 1).reshape(shape)


def shards(
    hidden, segment_ids, first_gain, second_gain, qkv_master, out_master, up_master, down_master
):
    lanes = lax.axis_size("tensor")
    groups = lax.axis_size("dp")
    shard_rows = qkv_master.shape[0]
    qkv_half = qkv_master.astype(jnp.bfloat16)
    up_half = up_master.astype(jnp.bfloat16).reshape(shard_rows, 1, up_master.shape[1])
    qkv_rows, up_rows = (
        lax.all_gather(qkv_half, "dp", axis=0, tiled=True),
        lax.all_gather(up_half, "dp", axis=0, tiled=True),
    )
    qkv_mixed, up_mixed = (
        lax.all_to_all(qkv_rows, "tensor", split_axis=2, concat_axis=0, tiled=True),
        lax.all_to_all(up_rows, "tensor", split_axis=2, concat_axis=0, tiled=True),
    )
    qkv_block = reorder(qkv_mixed, groups, lanes)
    up_joined = reorder(up_mixed, groups, lanes)
    up_block = up_joined.reshape(up_joined.shape[0], up_joined.shape[2])
    out_rows, down_rows = (
        lax.all_to_all(
            out_master.astype(jnp.bfloat16), "tensor", split_axis=0, concat_axis=1, tiled=True
        ),
        lax.all_to_all(
            down_master.astype(jnp.bfloat16), "tensor", split_axis=0, concat_axis=1, tiled=True
        ),
    )
    out_block, down_block = (
        lax.all_gather(out_rows, "dp", axis=1, tiled=True),
        lax.all_gather(down_rows, "dp", axis=1, tiled=True),
    )
    length = hidden.shape[0]
    own_count = length // lanes
    own_start = lax.axis_index("tensor") * own_count
    own_rows = lax.dynamic_slice_in_dim(hidden, own_start, own_count, 0)
    gathered = layer_norm(hidden, first_gain).astype(jnp.bfloat16)
    projected = jnp.einsum(
        "nd,dkc->nkc", gathered, qkv_block, preferred_element_type=jnp.float32
    ).astype(jnp.bfloat16)
    local_heads = qkv_block.shape[2] // HD
    all_heads = D // HD
    queries = projected[:, 0]
    key_rows = projected[:, 1]
    value_rows = projected[:, 2]
    head_index = lax.axis_index("tensor") * local_heads + jnp.arange(local_heads)
    slopes = jnp.exp2(-8.0 * (head_index.astype(jnp.float32) + 1.0) / all_heads)
    position = jnp.arange(length)
    distance = (position[:, None] - position[None, :]).astype(jnp.float32)
    allowed = (segment_ids[:, None] == segment_ids[None, :]) & (distance >= 0)
    scores = jnp.einsum(
        "qhe,khe->hqk",
        queries.reshape(length, local_heads, HD),
        key_rows.reshape(length, local_heads, HD),
        preferred_element_type=jnp.float32,
    ) / math.sqrt(HD)
    scores = scores - slopes[:, None, None] * distance
    scores = jnp.where(allowed, scores, -jnp.inf)
    highest = jnp.max(scores, axis=-1, keepdims=True)
    raised = jnp.exp(scores - highest)
    weights = (raised / jnp.sum(raised, axis=-1, keepdims=True)).astype(jnp.bfloat16)
    context = (
        jnp.einsum(
            "hqk,khe->qhe",
            weights,
            value_rows.reshape(length, local_heads, HD),
            preferred_element_type=jnp.float32,
        )
        .astype(jnp.bfloat16)
        .reshape(length, local_heads * HD)
    )
    attended = lax.psum_scatter(
        jnp.dot(context, out_block, preferred_element_type=jnp.float32).astype(jnp.bfloat16),
        "tensor",
        scatter_dimension=0,
        tiled=True,
    ).astype(jnp.float32)
    middle = (own_rows.astype(jnp.float32) + attended).astype(jnp.bfloat16)
    normed_two = layer_norm(middle, second_gain).astype(jnp.bfloat16)
    activated = jax.nn.gelu(
        jnp.dot(
            lax.all_gather(normed_two, "tensor", axis=0, tiled=True),
            up_block,
            preferred_element_type=jnp.float32,
        ),
        approximate=False,
    ).astype(jnp.bfloat16)
    lowered = lax.psum_scatter(
        jnp.dot(activated, down_block, preferred_element_type=jnp.float32).astype(jnp.bfloat16),
        "tensor",
        scatter_dimension=0,
        tiled=True,
    ).astype(jnp.float32)
    new_hidden = (middle.astype(jnp.float32) + lowered).astype(jnp.bfloat16)
    return (new_hidden, key_rows, value_rows, qkv_block, out_block, up_block, down_block)


def solution(mesh):
    in_specs = (
        P("dp", None),
        P("dp"),
        P(),
        P(),
        P(("dp", "tensor"), None, None),
        P(None, ("dp", "tensor")),
        P(("dp", "tensor"), None),
        P(None, ("dp", "tensor")),
    )
    out_specs = (
        P(("dp", "tensor"), None),
        P("dp", "tensor"),
        P("dp", "tensor"),
        P(None, None, "tensor"),
        P("tensor", None),
        P(None, "tensor"),
        P("tensor", None),
    )
    return jax.shard_map(shards, mesh=mesh, in_specs=in_specs, out_specs=out_specs, check_vma=False)
```

profile of v0, /device:TPU:0, one launch (start us, length us, event | category | flops | bytes accessed | tf_op | source)
XLA Modules:
  0.0 819.1 jit_solution(16999974862977725718)
XLA Ops:
  7.2 2.4 convert_element_type.77
  9.6 1.8 copy_bitcast_fusion.1
  11.4 10.7 %all-to-all-start.1 = ((bf16[32,128,32]{1,2,0:T(8,128)(2,1)}), bf16[32,128,32]{1,2,0:T(8,128)(2,1)S(1)}, u32[]{:S(2)}, u32[]{:S(2)}) async-start(bf16[32,128,32]{1,2,0:T(8,128)(2,1)} %copy_bitcast_fusion.1), calls=%async_computation.1 | async-start | bytes 524288 | tf_op jit(solution)/shard_map/all_to_all | solution.py:49
  22.1 31.0 %all-gather.7.cloned.1.call-done = bf16[128,3,4096]{2,0,1:T(8,128)(2,1)} async-done(((bf16[32,3,4096]{2,0,1:T(8,128)(2,1)}), bf16[128,3,4096]{2,0,1:T(8,128)(2,1)}) %all-gather.7.cloned.1.call-update) | async-done | bytes 3145744 | tf_op jit(solution)/shard_map/all_gather | solution.py:38
  53.1 7.1 copy.36
  60.2 0.7 copy-done.5
  60.9 9.3 %all-to-all-start = ((bf16[128,3,4096]{0,1,2:T(4,128)(2,1)}), bf16[128,3,4096]{0,1,2:T(4,128)(2,1)}, u32[]{:S(2)}, u32[]{:S(2)}) async-start(bf16[128,3,4096]{0,1,2:T(4,128)(2,1)} %copy.36), calls=%async_computation | async-start | bytes 8388608 | tf_op jit(solution)/shard_map/all_to_all | solution.py:42
  70.3 0.0 all-gather.9.cloned.1.call-start
  70.4 3.0 convert_reduce_fusion
  73.4 0.5 copy-done
  73.8 1.2 fusion.2
  75.1 0.0 reduce-scatter.3.cloned.1.call-start
  75.1 57.7 %all-to-all-done = bf16[128,3,4096]{0,1,2:T(4,128)(2,1)} async-done(((bf16[128,3,4096]{0,1,2:T(4,128)(2,1)}), bf16[128,3,4096]{0,1,2:T(4,128)(2,1)}, u32[]{:S(2)}, u32[]{:S(2)}) %all-to-all-start) | async-done | bytes 3145760 | tf_op jit(solution)/shard_map/all_to_all | solution.py:42
  132.9 2.6 copy.37
  135.5 2.8 copy.38
  138.3 2.7 copy.39
  141.0 0.4 copy-done.1
  141.4 2.4 fusion.10
  143.9 0.5 fusion.97
  144.4 0.2 fusion.25
  144.6 5.0 convolution_convert_fusion
  149.6 0.0 all-gather.15.cloned.1.call-start
  149.7 1.1 convert_element_type.91
  150.8 0.0 all-gather.13.cloned.1.call-start
  150.9 1.7 convert_element_type.93
  152.6 0.1 copy.55
  152.7 26.4 %all_to_all.68 = bf16[32,512,32]{1,2,0:T(8,128)(2,1)} all-to-all(bf16[32,512,32]{1,2,0:T(8,128)(2,1)S(1)} %bitcast.72), channel_id=1, replica_groups=mesh['dp'=4,'tensor'=32] {'tensor'}, dimensions={0} | all-to-all | bytes 2097152 | tf_op jit(solution)/shard_map/all_to_all | solution.py:52
  179.2 165.4 %reduce-scatter.3.cloned.1.call-done = bf16[16,4096]{1,0:T(8,128)(2,1)} async-done(((bf16[512,4096]{1,0:T(8,128)(2,1)}), bf16[16,4096]{1,0:T(8,128)(2,1)}) %reduce-scatter.3.cloned.1.call-update) | async-done | bytes 131088 | tf_op jit(solution)/shard_map/reduce_scatter | solution.py:99
  344.6 1.1 convert_reduce_fusion.1
  345.7 0.2 fusion.63
  346.0 0.8 fusion.65
  346.7 0.2 reduce-scatter.5.cloned.1.call-start
  347.0 41.2 %all-gather.15.cloned.1.call-done = bf16[128,16384]{1,0:T(8,128)(2,1)} async-done(((bf16[32,16384]{1,0:T(8,128)(2,1)}), bf16[128,16384]{1,0:T(8,128)(2,1)}) %all-gather.15.cloned.1.call-update) | async-done | bytes 4194320 | tf_op jit(solution)/shard_map/all_gather | solution.py:39
  388.1 17.8 %copy.41 = bf16[128,1,16384]{0,1,2:T(2,128)(2,1)} copy(bf16[128,1,16384]{2,0,1:T(8,128)(2,1)} %bitcast.67) | data formatting | bytes 8388608 | tf_op jit(solution)/shard_map/all_gather | solution.py:39
  406.0 0.5 broadcast.84
  406.5 90.7 %reduce.4 = bf16[16384,128]{1,0:T(8,128)(2,1)} reduce(bf16[16384,1,128]{2,1,0:T(2,128)(2,1)} %bitcast.61, bf16[]{:T(256)} %broadcast.84), dimensions={1}, to_apply=%bitcast.48.reduce_sub_computation | reduce | bytes 8388610
  497.2 6.9 reshape.117
  504.1 65.8 %all_to_all.69 = bf16[32,2,32768]{2,1,0:T(2,128)(2,1)} all-to-all(bf16[32,2,32768]{2,1,0:T(2,128)(2,1)} %reshape.117), channel_id=1, replica_groups=mesh['dp'=4,'tensor'=32] {'tensor'}, dimensions={0} | all-to-all | bytes 8388608 | tf_op jit(solution)/shard_map/all_to_all | solution.py:43
  569.9 19.8 %reshape.118 = bf16[16384,1,128]{2,1,0:T(2,128)(2,1)} reshape(bf16[32,2,32768]{2,1,0:T(2,128)(2,1)} %all_to_all.69) | data formatting | bytes 8388608
  589.7 5.9 copy.50
  595.5 6.5 copy.42
  602.0 4.8 copy.43
  606.8 13.4 %convolution_convert_fusion.1 = bf16[512,4096]{1,0:T(8,128)(2,1)} fusion(bf16[512,4096]{0,1:T(8,128)(2,1)} %all-gather.13.cloned.1.call-done, bf16[512,4096]{1,0:T(8,128)(2,1)} %all-gather.11.cloned.1.call-done, bf16[4096,512]{1,0:T(8,128)(2,1)} %bitcast.69), kind=kOutput, calls=%fused_computation.8 | convolution fusion | flops 4314103808 | bytes 16777216 | tf_op jit(solution)/shard_map/dot_general | solution.py:116
  620.2 1.2 copy-done.2
  621.4 1.3 copy.47
  622.7 6.3 copy.48
  629.1 181.6 %reduce-scatter.5.cloned.1.call-done = bf16[16,4096]{1,0:T(8,128)(2,1)} async-done(((bf16[512,4096]{1,0:T(8,128)(2,1)}), bf16[16,4096]{1,0:T(8,128)(2,1)}) %reduce-scatter.5.cloned.1.call-update) | async-done | bytes 131088 | tf_op jit(solution)/shard_map/reduce_scatter | solution.py:115
  810.6 1.6 fusion.66
  (36 shorter events, 0.3 us)
Async XLA Ops:
  7.2 45.9 %all-gather.7.cloned.1.call-start = ((), (), s32[]{:S(2)}) async-start(), calls=%async_computation.6 | async-start | bytes 3932160 | tf_op jit(solution)/shard_map/all_gather | solution.py:38
  11.4 48.8 %all-to-all-start.1 = ((bf16[32,128,32]{1,2,0:T(8,128)(2,1)}), bf16[32,128,32]{1,2,0:T(8,128)(2,1)S(1)}, u32[]{:S(2)}, u32[]{:S(2)}) async-start(bf16[32,128,32]{1,2,0:T(8,128)(2,1)} %copy_bitcast_fusion.1), calls=%async_computation.1 | async-start | bytes 524288 | tf_op jit(solution)/shard_map/all_to_all | solution.py:49
  60.2 0.7 copy-start.5
  60.9 71.9 %all-to-all-start = ((bf16[128,3,4096]{0,1,2:T(4,128)(2,1)}), bf16[128,3,4096]{0,1,2:T(4,128)(2,1)}, u32[]{:S(2)}, u32[]{:S(2)}) async-start(bf16[128,3,4096]{0,1,2:T(4,128)(2,1)} %copy.36), calls=%async_computation | async-start | bytes 8388608 | tf_op jit(solution)/shard_map/all_to_all | solution.py:42
  70.3 74.3 %all-gather.9.cloned.1.call-start = ((), (), s32[]{:S(2)}) async-start(), calls=%async_computation.7 | async-start | bytes 1310720 | tf_op jit(solution)/shard_map/all_gather | solution.py:57
  70.4 3.5 copy-start
  75.1 269.5 %reduce-scatter.3.cloned.1.call-start = ((), (), s32[]{:S(2)}) async-start(), calls=%async_computation.8 | async-start | bytes 4325376 | tf_op jit(solution)/shard_map/reduce_scatter | solution.py:99
  138.3 3.1 copy-start.1
  138.3 3.1 copy-start.9
  141.0 2.8 copy-start.3
  141.4 2.5 copy-start.10
  143.8 5.8 copy-start.6
  143.8 5.8 copy-start.7
  144.6 5.1 copy-start.4
  149.6 238.5 %all-gather.15.cloned.1.call-start = ((), (), s32[]{:S(2)}) async-start(), calls=%async_computation.12 | async-start | bytes 5242880 | tf_op jit(solution)/shard_map/all_gather | solution.py:39
  150.8 195.1 %copy-start.8 = (f32[4096]{0:T(1024)S(1)}, f32[4096]{0:T(1024)}, u32[]{:S(2)}) copy-start(f32[4096]{0:T(1024)} %param.11) | copy-start | bytes 49156
  150.8 456.0 %all-gather.13.cloned.1.call-start = ((), (), s32[]{:S(2)}) async-start(), calls=%async_computation.10 | async-start | bytes 5242880 | tf_op jit(solution)/shard_map/all_gather | solution.py:58
  179.1 427.7 %all-gather.11.cloned.1.call-start = ((), (), s32[]{:S(2)}) async-start(), calls=%async_computation.9 | async-start | bytes 4325376 | tf_op jit(solution)/shard_map/all_gather | solution.py:109
  346.7 463.9 %reduce-scatter.5.cloned.1.call-start = ((), (), s32[]{:S(2)}) async-start(), calls=%async_computation.11 | async-start | bytes 4325376 | tf_op jit(solution)/shard_map/reduce_scatter | solution.py:115
  620.2 1.2 copy-start.2
Sparse Core Ops, SparseCore 0:
  10.2 42.7 all-gather.6
  75.2 50.0 all-gather.8
  149.8 194.7 reduce-scatter.2
  346.7 41.4 all-gather.14
  389.6 47.4 all-gather.12
  440.7 109.3 all-gather.10
  620.4 190.2 reduce-scatter.4
where the time goes:
time: 821 us; the launch traced here: 819 us
  waiting for transfers between devices  477 us (58%)
  other arithmetic  106 us (13%)
  blocking collectives  92.2 us (11%)
  local copies, waits for them, and re-layouts  88 us (11%)
  matrix products  21.3 us (3%)
  starting transfers between devices  20.5 us (2%)
  between operations  14.3 us (2%)
    reduce_scatter x1, waiting for transfers between devices, shards(): lax.psum_scatter(jnp.dot(activated, down_block, preferred_element_type=jn...  182 us
    reduce_scatter x1, waiting for transfers between devices, shards(): lax.psum_scatter(jnp.dot(context, out_block, preferred_element_type=jnp.f...  165 us
    unnamed x1, other arithmetic  90.7 us
    all_to_all x1, blocking collectives, shards(): lax.all_to_all(up_rows, 'tensor', split_axis=2, concat_axis=0, tiled=True)  65.8 us
    all_to_all x1, waiting for transfers between devices, shards(): lax.all_to_all(qkv_rows, 'tensor', split_axis=2, concat_axis=0, tiled=True)  57.7 us
    unnamed x28, local copies, waits for them, and re-layouts  43.5 us
    all_gather x1, waiting for transfers between devices, shards(): lax.all_gather(up_half, 'dp', axis=0, tiled=True)  41.2 us
    all_gather x1, waiting for transfers between devices, shards(): lax.all_gather(qkv_half, 'dp', axis=0, tiled=True)  31 us
  transfers between devices with their start and end apart: 9, of which 5 were waited for; matrix products, arithmetic and copies ran while one was open for 23% of the time, Pallas kernels for 0%

commit v1 on v0

v1 whole, which is shorter than its diff:
```python
import functools
import math

import jax
import jax.numpy as jnp
from jax import lax
from jax.experimental import pallas as pl
from jax.experimental.pallas import tpu as pltpu
from jax.sharding import PartitionSpec as P

D = 4096
HD = 128
EPSILON = 1e-05
MESH = pl.DeviceIdType.MESH
BF16 = jnp.bfloat16
F32 = jnp.float32


def layer_norm(values, gain):
    values = values.astype(F32)
    center = values - jnp.mean(values, axis=-1, keepdims=True)
    spread = jnp.mean(center * center, axis=-1, keepdims=True)
    return center * lax.rsqrt(spread + EPSILON) * gain


class Place:
    def __init__(self):
        self.dp = lax.axis_index("dp")
        self.t = lax.axis_index("tensor")
        self.zl = self.dp // 2
        self.core = self.dp % 2
        self.x = self.t // 8
        self.zh = (self.t // 4) % 2
        self.y = self.t % 4
        self.z_pair = (1 - self.zl) * 2 + self.core
        self.core_pair = self.zl * 2 + (1 - self.core)

    def near(self, axis, delta):
        if axis == "x":
            return (self.dp, ((self.x + delta) % 4) * 8 + self.zh * 4 + self.y)
        return (self.dp, self.x * 8 + self.zh * 4 + (self.y + delta) % 4)

    def across(self):
        return (self.dp, self.x * 8 + (1 - self.zh) * 4 + self.y)


def remote(src, dst, send_sem, recv_sem, device):
    return pltpu.make_async_remote_copy(
        src_ref=src,
        dst_ref=dst,
        send_sem=send_sem,
        recv_sem=recv_sem,
        device_id=device,
        device_id_type=MESH,
    )


def greet(barrier, device):
    pl.semaphore_signal(barrier, inc=1, device_id=device, device_id_type=MESH)


def relay_kernel(
    q_in, o_in, u_in, w_in, qo, upq, dnq, sq, su, sw, local, s_sem, r_sem, fz_s, fz_r, fc_s, fc_r, f3_s, f3_r
):
    me = Place()

    def holder(step):
        other = (me.t + step) % 32
        apart = (me.zh + (other // 4) % 2) % 2
        return other, apart, ((me.zl + apart) % 2) * 2 + me.core

    barrier = pltpu.get_barrier_semaphore()

    def hello(step, carry):
        other, _, group = holder(step)
        greet(barrier, (group, other))
        return carry

    lax.fori_loop(1, 32, hello, 0)
    greet(barrier, (me.z_pair, me.t))
    greet(barrier, (me.core_pair, me.t))

    sq[0:3] = q_in[...].astype(BF16)
    sq[3] = o_in[...].astype(BF16)
    pl.semaphore_wait(barrier, 33)

    mine = me.dp * 8 + me.x * 2 + me.zh
    rows = pl.ds(pl.multiple_of(me.y * 32, 32), 32)

    def send(source, place, index):
        def body(step, carry):
            other, apart, group = holder(step)
            slot = apart * 4 + me.x
            remote(
                source(other), place(slot), s_sem.at[index], r_sem.at[index * 8 + slot], (group, other)
            ).start()
            return carry

        lax.fori_loop(1, 32, body, 0)
        own = pltpu.make_async_copy(source(me.t), place(me.x), local.at[index])
        own.start()
        return own

    def cut(ref, wide):
        return lambda other: ref.at[..., pl.ds(pl.multiple_of(other * wide, wide), wide)]

    own_q = send(cut(sq, 128), lambda slot: qo.at[:, mine, rows, :], 0)

    @pl.loop(0, 4)
    def _(part):
        cols = pl.ds(pl.multiple_of(part * 4096, 4096), 4096)
        su[:, cols] = u_in[:, cols].astype(BF16)

    own_u = send(cut(su, 512), lambda slot: upq.at[slot, rows, :], 1)

    @pl.loop(0, 4)
    def _(part):
        cols = pl.ds(pl.multiple_of(part * 4096, 4096), 4096)
        sw[:, cols] = w_in[:, cols].astype(BF16)

    own_w = send(cut(sw, 512), lambda slot: dnq.at[slot, rows, :], 2)
    own_q.wait()
    own_u.wait()
    own_w.wait()

    def batch(slot, flip_z, flip_c):
        apart = slot // 4
        zl = (me.zl + apart + flip_z) % 2
        core = (me.core + flip_c) % 2
        return (zl * 2 + core) * 8 + (slot % 4) * 2 + (me.zh + apart) % 2

    def wait_pieces(base, row_ref, slot):
        full = row_ref(slot)

        @pl.when(slot != me.x)
        def _():
            remote(full(128), full(128), s_sem.at[0], r_sem.at[base + slot], (me.core_pair, me.t)).wait_recv()

        @pl.when(slot == me.x)
        def _():
            remote(full(96), full(96), s_sem.at[0], r_sem.at[base + slot], (me.core_pair, me.t)).wait_recv()

    def q_rows(slot):
        return lambda count: qo.at[:, batch(slot, 0, 0), pl.ds(0, count), :]

    def to_z(slot):
        ref = qo.at[:, batch(slot, 0, 0)]
        return remote(ref, ref, fz_s.at[slot], fz_r.at[slot], (me.z_pair, me.t))

    def to_core(slot):
        ref = qo.at[:, batch(slot, 0, 0)]
        return remote(ref, ref, fc_s.at[slot], fc_r.at[slot], (me.core_pair, me.t))

    def pass_on(slot):
        ref = qo.at[:, batch(slot, 1, 0)]
        return remote(ref, ref, f3_s.at[slot], f3_r.at[slot], (me.core_pair, me.t))

    def got(slot, flip_z, flip_c, sem):
        ref = qo.at[:, batch(slot, flip_z, flip_c)]
        remote(ref, ref, s_sem.at[0], sem, (me.core_pair, me.t)).wait_recv()

    lag = 2

    def forward(step, carry):
        @pl.when(step < 8)
        def _():
            wait_pieces(0, q_rows, step)
            to_z(step).start()
            to_core(step).start()

        @pl.when(step >= lag)
        def _():
            got(step - lag, 1, 0, fz_r.at[step - lag])
            pass_on(step - lag).start()

        return carry

    lax.fori_loop(0, 8 + lag, forward, 0)

    def finish(slot, carry):
        wait_pieces(8, lambda s: lambda count: upq.at[s, pl.ds(0, count), :], slot)
        wait_pieces(16, lambda s: lambda count: dnq.at[s, pl.ds(0, count), :], slot)
        got(slot, 0, 1, fc_r.at[slot])
        got(slot, 1, 1, f3_r.at[slot])
        to_z(slot).wait_send()
        to_core(slot).wait_send()
        pass_on(slot).wait_send()
        return carry

    lax.fori_loop(0, 8, finish, 0)
    for index, ref, wide in ((0, sq, 128), (1, su, 512), (2, sw, 512)):
        sent = ref.at[..., pl.ds(0, 31 * wide)]
        remote(sent, sent, s_sem.at[index], r_sem.at[0], (me.core_pair, me.t)).wait_send()


def relay(qkv, out, up, down):
    any_spec = pl.BlockSpec(memory_space=pl.ANY)
    dma = pltpu.SemaphoreType.DMA
    return pl.pallas_call(
        relay_kernel,
        out_shape=(
            jax.ShapeDtypeStruct((4, 32, 128, 128), BF16),
            jax.ShapeDtypeStruct((8, 128, 512), BF16),
            jax.ShapeDtypeStruct((8, 128, 512), BF16),
        ),
        in_specs=[pl.BlockSpec(memory_space=pltpu.VMEM)] * 4,
        out_specs=[any_spec] * 3,
        scratch_shapes=[
            pltpu.VMEM((4, 32, 4096), BF16),
            pltpu.VMEM((32, 16384), BF16),
            pltpu.VMEM((32, 16384), BF16),
            dma((3,)),
            dma((3,)),
            dma((24,)),
        ]
        + [dma((8,))] * 6,
        compiler_params=pltpu.CompilerParams(
            collective_id=0, has_side_effects=True, vmem_limit_bytes=48 << 20
        ),
        name="relay",
    )(qkv, out, up, down)


HALF = 2048


def reduce_rows(me, share, bufs, sems):
    ra, acc_a, rb, acc_b, kept, last, last_half, rc = bufs
    sa, qa, sb, qb, sc, qc = sems
    axes = (("x", "y"), ("y", "x"))

    def chunk_a(f, q, h):
        if f == 0:
            return share.at[q, h, :, :, pl.ds(0, HALF)]
        return share.at[:, h, q, :, pl.ds(HALF, HALF)]

    def chunk_b(f, q, h):
        return kept.at[f, q, h]

    def position(axis):
        return me.x if axis == "x" else me.y

    def stage(level, chunk, recv, acc, s_sem, r_sem, store):
        started = []
        plan = []
        for f in range(2):
            axis = axes[f][level]
            p = position(axis)
            far = (p + 2) % 4
            for way in range(2):
                delta = 1 - 2 * way
                near = (p + delta) % 4
                device = me.near(axis, delta)
                first = remote(
                    chunk(f, far, way), recv.at[f, way, 0], s_sem.at[f, way, 0], r_sem.at[f, way, 0], device
                )
                plain = remote(
                    chunk(f, near, 1 - way), recv.at[f, way, 1], s_sem.at[f, way, 1], r_sem.at[f, way, 1], device
                )
                summed = remote(
                    acc.at[f, way], recv.at[f, way, 2], s_sem.at[f, way, 2], r_sem.at[f, way, 2], device
                )
                plan.append((f, way, near, first, plain, summed))
        for f, way, near, first, plain, summed in plan:
            first.start()
        for f, way, near, first, plain, summed in plan:
            plain.start()
        for f, way, near, first, plain, summed in plan:
            first.wait_recv()
            acc[f, way] = (chunk(f, near, way)[...].astype(F32) + recv[f, way, 0].astype(F32)).astype(BF16)
            summed.start()
        for f in range(2):
            p = position(axes[f][level])
            both = [entry for entry in plan if entry[0] == f]
            for h in range(2):
                both[1 - h][4].wait_recv()
                both[h][5].wait_recv()
                total = (
                    chunk(f, p, h)[...].astype(F32)
                    + recv[f, h, 2].astype(F32)
                    + recv[f, 1 - h, 1].astype(F32)
                )
                store(f, h, total)
        for f, way, near, first, plain, summed in plan:
            first.wait_send()
            plain.wait_send()
            summed.wait_send()

    def store_a(f, h, total):
        kept[f, :, h] = total.astype(BF16)

    def store_b(f, h, total):
        last[f, h] = total
        last_half[f, h] = total.astype(BF16)

    stage(0, chunk_a, ra, acc_a, sa, qa, store_a)
    stage(1, chunk_b, rb, acc_b, sb, qb, store_b)
    swaps = [
        remote(last_half.at[f, 1 - me.zh], rc.at[f], sc.at[f], qc.at[f], me.across()) for f in range(2)
    ]
    for swap in swaps:
        swap.start()
    sums = []
    for f, swap in enumerate(swaps):
        swap.wait_recv()
        sums.append(last[f, me.zh] + rc[f].astype(F32))
    for swap in swaps:
        swap.wait_send()
    return sums


def reduce_scratch():
    dma = pltpu.SemaphoreType.DMA
    bufs = [
        pltpu.VMEM((2, 2, 3, 4, 16, HALF), BF16),
        pltpu.VMEM((2, 2, 4, 16, HALF), BF16),
        pltpu.VMEM((2, 2, 3, 16, HALF), BF16),
        pltpu.VMEM((2, 2, 16, HALF), BF16),
        pltpu.VMEM((2, 4, 2, 16, HALF), BF16),
        pltpu.VMEM((2, 2, 16, HALF), F32),
        pltpu.VMEM((2, 2, 16, HALF), BF16),
        pltpu.VMEM((2, 16, HALF), BF16),
    ]
    sems = [dma((2, 2, 3)), dma((2, 2, 3)), dma((2, 2, 3)), dma((2, 2, 3)), dma((2,)), dma((2,))]
    return bufs, sems


def meet(me, pairs):
    barrier = pltpu.get_barrier_semaphore()
    around = [me.near("x", 1), me.near("x", -1), me.near("y", 1), me.near("y", -1), me.across()]
    if pairs:
        around += [(me.z_pair, me.t), (me.core_pair, me.t)]
    for device in around:
        greet(barrier, device)
    pl.semaphore_wait(barrier, len(around))


def middle_kernel(share, hidden, gain, upq, dnq, gathered, middle, up, down, *scratch):
    bufs, sems = scratch[:8], scratch[8:14]
    (field, rows, h_sem, z_s, z_r, c_s, c_r, p_s, p_r, own_sem, a_s, a_r, b_s, b_r, x_s, x_r, o_sem) = scratch[14:]
    me = Place()
    take = pltpu.make_async_copy(hidden.at[pl.ds(pl.multiple_of(me.t * 16, 16), 16), :], rows, h_sem)
    take.start()
    meet(me, True)

    def place(full, apart, flip_z, flip_c):
        zl = (me.zl + apart + flip_z) % 2
        core = (me.core + flip_c) % 2
        return full.at[zl * 2 + core, :, (me.zh + apart) % 2]

    moves = []
    for k, (quarter, full) in enumerate(((upq, up), (dnq, down))):
        for apart in range(2):
            n = 2 * k + apart
            src = quarter.at[pl.ds(4 * apart, 4)]
            dst = place(full, apart, 0, 0)
            to_z = remote(src, dst, z_s.at[n], z_r.at[n], (me.z_pair, me.t))
            to_c = remote(src, dst, c_s.at[n], c_r.at[n], (me.core_pair, me.t))
            own = pltpu.make_async_copy(src, dst, own_sem.at[n])
            came = place(full, apart, 1, 0)
            passed = remote(came, came, p_s.at[n], p_r.at[n], (me.core_pair, me.t))
            moves.append((to_z, to_c, own, passed))
    for to_z, to_c, own, passed in moves:
        to_z.start()
        to_c.start()
        own.start()

    left, right = reduce_rows(me, share, bufs, sems)
    take.wait()
    mid_l = (rows[:, :HALF].astype(F32) + left).astype(BF16)
    mid_r = (rows[:, HALF:].astype(F32) + right).astype(BF16)
    middle[:, :HALF] = mid_l
    middle[:, HALF:] = mid_r
    values = middle[...].astype(F32)
    center = values - jnp.mean(values, axis=-1, keepdims=True)
    spread = jnp.mean(center * center, axis=-1, keepdims=True)
    field[me.x, me.zh, me.y] = (center * lax.rsqrt(spread + EPSILON) * gain[...]).astype(BF16)

    swap = remote(
        field.at[me.x, me.zh, me.y], field.at[me.x, me.zh, me.y], x_s, x_r, me.across()
    )
    swap.start()
    swap.wait_recv()

    def view_b(f, q, h):
        cols = pl.ds(f * HALF, HALF)
        lane = slice(None) if h is None else h
        if f == 0:
            return field.at[me.x, lane, q, :, cols]
        return field.at[q, lane, me.y, :, cols]

    def view_a(f, q, h):
        cols = pl.ds(f * HALF, HALF)
        lane = slice(None) if h is None else h
        if f == 0:
            return field.at[q, lane, :, :, cols]
        return field.at[:, lane, q, :, cols]

    def spread_out(view, axes, s_sem, r_sem):
        plan = []
        for f in range(2):
            axis = axes[f]
            p = me.x if axis == "x" else me.y
            for way in range(2):
                delta = 1 - 2 * way
                device = me.near(axis, delta)
                unit = view(f, p, None)
                came = view(f, (p + 4 - delta) % 4, way)
                plan.append(
                    (
                        remote(unit, unit, s_sem.at[f, way, 0], r_sem.at[f, way, 0], device),
                        remote(came, came, s_sem.at[f, way, 1], r_sem.at[f, way, 1], device),
                    )
                )
        for whole, half in plan:
            whole.start()
        for whole, half in plan:
            whole.wait_recv()
            half.start()
        for whole, half in plan:
            half.wait_recv()
        for whole, half in plan:
            whole.wait_send()
            half.wait_send()

    spread_out(view_b, ("y", "x"), b_s, b_r)
    for to_z, to_c, own, passed in moves[:2]:
        to_z.wait_recv()
        passed.start()
    spread_out(view_a, ("x", "y"), a_s, a_r)
    write = pltpu.make_async_copy(field, gathered, o_sem)
    write.start()
    for to_z, to_c, own, passed in moves[2:]:
        to_z.wait_recv()
        passed.start()
    swap.wait_send()
    for to_z, to_c, own, passed in moves:
        to_c.wait_recv()
        passed.wait_recv()
        own.wait()
        to_z.wait_send()
        to_c.wait_send()
        passed.wait_send()
    write.wait()


def middle_step(share, hidden, gain, upq, dnq):
    dma = pltpu.SemaphoreType.DMA
    bufs, sems = reduce_scratch()
    any_spec = pl.BlockSpec(memory_space=pl.ANY)
    vmem = pl.BlockSpec(memory_space=pltpu.VMEM)
    return pl.pallas_call(
        middle_kernel,
        out_shape=(
            jax.ShapeDtypeStruct((4, 2, 4, 16, D), BF16),
            jax.ShapeDtypeStruct((16, D), BF16),
            jax.ShapeDtypeStruct((4, 4, 2, 128, 512), BF16),
            jax.ShapeDtypeStruct((4, 4, 2, 128, 512), BF16),
        ),
        in_specs=[vmem, any_spec, vmem, any_spec, any_spec],
        out_specs=[any_spec, vmem, any_spec, any_spec],
        scratch_shapes=bufs
        + sems
        + [pltpu.VMEM((4, 2, 4, 16, D), BF16), pltpu.VMEM((16, D), BF16), dma(())]
        + [dma((4,))] * 7
        + [dma((2, 2, 2))] * 4
        + [dma(()), dma(()), dma(())],
        compiler_params=pltpu.CompilerParams(
            collective_id=1, has_side_effects=True, vmem_limit_bytes=48 << 20
        ),
        name="middle",
    )(share.reshape(4, 2, 4, 16, D), hidden, gain.reshape(1, D), upq, dnq)


def last_kernel(share, middle, result, *scratch):
    bufs, sems = scratch[:8], scratch[8:14]
    me = Place()
    meet(me, False)
    left, right = reduce_rows(me, share, bufs, sems)
    result[:, :HALF] = (middle[:, :HALF].astype(F32) + left).astype(BF16)
    result[:, HALF:] = (middle[:, HALF:].astype(F32) + right).astype(BF16)


def last_step(share, middle):
    bufs, sems = reduce_scratch()
    vmem = pl.BlockSpec(memory_space=pltpu.VMEM)
    return pl.pallas_call(
        last_kernel,
        out_shape=jax.ShapeDtypeStruct((16, D), BF16),
        in_specs=[vmem, vmem],
        out_specs=vmem,
        scratch_shapes=bufs + sems,
        compiler_params=pltpu.CompilerParams(
            collective_id=2, has_side_effects=True, vmem_limit_bytes=48 << 20
        ),
        name="last",
    )(share.reshape(4, 2, 4, 16, D), middle)


def shards(
    hidden, segment_ids, first_gain, second_gain, qkv_master, out_master, up_master, down_master
):
    qo, upq, dnq = relay(qkv_master.transpose(1, 0, 2), out_master.T, up_master, down_master.T)
    qo = qo.reshape(4, D, HD)
    qkv = qo[:3]
    out_t = qo[3]
    normed = layer_norm(hidden, first_gain).astype(BF16)
    projected = jnp.einsum("nd,kdc->knc", normed, qkv, preferred_element_type=F32).astype(BF16)
    queries, key_rows, value_rows = projected[0], projected[1], projected[2]
    length = hidden.shape[0]
    slope = jnp.exp2(-8.0 * (lax.axis_index("tensor").astype(F32) + 1.0) / (D // HD))
    position = jnp.arange(length)
    distance = (position[:, None] - position[None, :]).astype(F32)
    allowed = (segment_ids[:, None] == segment_ids[None, :]) & (distance >= 0)
    scores = lax.dot_general(
        queries, key_rows, (((1,), (1,)), ((), ())), preferred_element_type=F32
    ) / math.sqrt(HD)
    scores = jnp.where(allowed, scores - slope * distance, -jnp.inf)
    highest = jnp.max(scores, axis=-1, keepdims=True)
    raised = jnp.exp(scores - highest)
    weights = (raised / jnp.sum(raised, axis=-1, keepdims=True)).astype(BF16)
    context = jnp.dot(weights, value_rows, preferred_element_type=F32).astype(BF16)
    share = lax.dot_general(
        context, out_t, (((1,), (1,)), ((), ())), preferred_element_type=F32
    ).astype(BF16)
    gathered, middle, up, down = middle_step(share, hidden, second_gain, upq, dnq)
    up = up.reshape(D, 512)
    down_t = down.reshape(D, 512)
    activated = jax.nn.gelu(
        jnp.dot(gathered.reshape(512, D), up, preferred_element_type=F32), approximate=False
    ).astype(BF16)
    share_two = lax.dot_general(
        activated, down_t, (((1,), (1,)), ((), ())), preferred_element_type=F32
    ).astype(BF16)
    new_hidden = last_step(share_two, middle)
    return (
        new_hidden,
        key_rows,
        value_rows,
        qkv.transpose(1, 0, 2),
        out_t.T,
        up,
        down_t.T,
    )


def solution(mesh):
    in_specs = (
        P("dp", None),
        P("dp"),
        P(),
        P(),
        P(("dp", "tensor"), None, None),
        P(None, ("dp", "tensor")),
        P(("dp", "tensor"), None),
        P(None, ("dp", "tensor")),
    )
    out_specs = (
        P(("dp", "tensor"), None),
        P("dp", "tensor"),
        P("dp", "tensor"),
        P(None, None, "tensor"),
        P("tensor", None),
        P(None, "tensor"),
        P("tensor", None),
    )
    return jax.shard_map(shards, mesh=mesh, in_specs=in_specs, out_specs=out_specs, check_vma=False)
```

time: 821 us -> 233 us (0.28)
  waiting for transfers between devices: 477 us -> 0 us
  Pallas kernels: 0 us -> 186 us
  other arithmetic: 106 us -> 4.4 us
  blocking collectives: 92.2 us -> 0 us
  local copies, waits for them, and re-layouts: 88 us -> 19.8 us
  starting transfers between devices: 20.5 us -> 0 us
  between operations: 14.3 us -> 0.85 us
    reduce_scatter x2 -> x0, waiting for transfers between devices: 347 us -> none  [the longest x1 182 us: shards(): lax.psum_scatter(jnp.dot(activated, down_block, preferred_element_type=jn...]
    pallas_call x0 -> x3, Pallas kernels: none -> 186 us  [the longest x1 100 us: middle_step(): pl.pallas_call(middle_kernel, out_shape=(jax.ShapeDtypeStruct((4, 2, 4, 1...]
    all_to_all x2 -> x0, blocking collectives: 92.2 us -> none  [the longest x1 65.8 us: shards(): lax.all_to_all(up_rows, 'tensor', split_axis=2, concat_axis=0, tiled=True)]
    unnamed x1 -> x0, other arithmetic: 90.7 us -> none
    all_gather x5 -> x0, waiting for transfers between devices: 72.1 us -> none  [the longest x1 41.2 us: shards(): lax.all_gather(up_half, 'dp', axis=0, tiled=True)]
    all_to_all x2 -> x0, waiting for transfers between devices: 57.7 us -> none  [the longest x1 57.7 us: shards(): lax.all_to_all(qkv_rows, 'tensor', split_axis=2, concat_axis=0, tiled=True)]
    unnamed x28 -> x26, local copies, waits for them, and re-layouts: 43.5 us -> 8.54 us
    all_gather x2 -> x0, local copies, waits for them, and re-layouts: 25 us -> none  [the longest x1 17.8 us: shards(): lax.all_gather(up_half, 'dp', axis=0, tiled=True)]
  transfers between devices with their start and end apart: 9 -> 0, of which waited for: 5 -> 0; matrix products, arithmetic and copies ran while one was open for 23% -> 0% of each run, Pallas kernels for 0% -> 0%
where the time goes in v1:
time: 233 us
  Pallas kernels  186 us (80%)
  matrix products  21.9 us (9%)
  local copies, waits for them, and re-layouts  19.8 us (8%)
  other arithmetic  4.4 us (2%)
    pallas_call x1, Pallas kernels, middle_step(): pl.pallas_call(middle_kernel, out_shape=(jax.ShapeDtypeStruct((4, 2, 4, 1...  100 us
    pallas_call x1, Pallas kernels, relay(): pl.pallas_call(relay_kernel, out_shape=(jax.ShapeDtypeStruct((4, 32, 128,...  49.3 us
    pallas_call x1, Pallas kernels, last_step(): pl.pallas_call(last_kernel, out_shape=jax.ShapeDtypeStruct((16, D), BF16)...  36.5 us
    dot_general x1, matrix products, shards(): lax.dot_general(activated, down_t, (((1,), (1,)), ((), ())), preferred_el...  13.5 us
    unnamed x26, local copies, waits for them, and re-layouts  8.54 us
    reshape x1, local copies, waits for them, and re-layouts, shards(): down_t = down.reshape(D, 512)  6.32 us
    dot_general x1, matrix products, shards(): lax.dot_general(context, out_t, (((1,), (1,)), ((), ())), preferred_eleme...  4.91 us

profile of v1, /device:TPU:0, one launch (start us, length us, event | category | flops | bytes accessed | tf_op | source)
XLA Modules:
  0.0 232.8 jit_solution(3048626559417396330)
XLA Ops:
  0.7 0.0 copy-start.4
  0.7 0.0 copy-start.1
  0.7 0.0 copy-start.2
  0.7 3.0 %convert_reduce_fusion = f32[512]{0:T(512)S(1)} fusion(bf16[512,4096]{1,0:T(8,128)(2,1)} %hidden.1), kind=kLoop, calls=%fused_computation.1 | loop fusion | flops 4193792 | bytes 4196352 | tf_op jit(solution)/shard_map/reduce_sum | solution.py:21
  3.7 0.4 copy-done.4
  4.1 1.2 fusion.2
  5.4 0.0 copy-done.1
  5.4 0.0 copy-done.2
  5.4 49.3 %relay.1 = (bf16[4,32,128,128]{3,2,1,0:T(8,128)(2,1)}, bf16[8,128,512]{2,1,0:T(8,128)(2,1)S(1)}, bf16[8,128,512]{2,1,0:T(8,128)(2,1)S(1)}) custom-call(f32[3,32,4096]{2,1,0:T(8,128)S(1)} %bitcast.44, f32[32,4096]{1,0:T(8,128)S(1)} %bitcast.45, f32[32,16384]{1,0:T(8,128)} %u_in.1, f32[32,16384]{1,0:T(8,128)} %bitcast.57), custom_call_target="tpu_custom_call" | custom-call | tf_op jit(solution)/shard_map/relay/pallas_call | solution.py:199
  54.7 0.0 copy-start.9
  54.7 1.3 slice.24
  56.0 2.3 slice.19
  58.3 0.0 copy-start.7
  58.3 0.0 copy-done.9
  58.4 0.0 copy-start.10
  58.4 2.0 fusion.13
  60.4 0.0 copy-done.7
  60.4 0.0 copy-start.8
  60.4 0.7 copy-done.8
  61.1 0.8 copy.21
  61.9 0.8 copy.20
  62.7 1.3 copy.18
  64.0 0.0 copy-done.10
  64.0 1.5 fusion.93
  65.5 0.0 copy-start.6
  65.5 0.0 copy-start.3
  65.5 1.0 copy-done.6
  66.5 0.2 fusion.27
  66.7 4.9 %convolution_convert_fusion = bf16[512,4096]{1,0:T(8,128)(2,1)} fusion(bf16[4096,128]{1,0:T(8,128)(2,1)S(1)} %bitcast.49, f32[512,512]{0,1:T(8,128)} %copy-done.6, f32[512]{0:T(512)S(1)} %fusion.27, f32[512]{0:T(512)S(1)} %get-tuple-element.30, bf16[3,512,128]{1,2,0:T(8,128)(2,1)} %copy-done.8), kind=kOutput, calls=%fused_computation.7 | convolution fusion | flops 606928896 | bytes 6426624 | tf_op jit(solution)/shard_map/dot_general | solution.py:523
  71.6 0.0 copy-done.3
  71.6 100.1 %middle.1 = (bf16[4,2,4,16,4096]{4,3,2,1,0:T(8,128)(2,1)}, bf16[16,4096]{1,0:T(8,128)(2,1)S(1)}, bf16[4,4,2,128,512]{4,3,2,1,0:T(8,128)(2,1)}, bf16[4,4,2,128,512]{4,3,2,1,0:T(8,128)(2,1)}) custom-call(bf16[4,2,4,16,4096]{4,3,2,1,0:T(8,128)(2,1)} %bitcast.47, bf16[512,4096]{1,0:T(8,128)(2,1)} %hidden.1, f32[1,4096]{1,0:T(1,128)S(1)} %bitcast.46, ...), custom_call_target="tpu_custom_call" | custom-call | tf_op jit(solution)/shard_map/middle/pallas_call | solution.py:452
  171.7 13.5 %convolution_convert_fusion.1 = bf16[512,4096]{1,0:T(8,128)(2,1)} fusion(bf16[4096,512]{1,0:T(8,128)(2,1)} %bitcast.53, bf16[512,4096]{1,0:T(8,128)(2,1)} %bitcast.59, bf16[4096,512]{1,0:T(8,128)(2,1)} %bitcast.51), kind=kOutput, calls=%fused_computation.8 | convolution fusion | flops 4314103808 | bytes 16777216 | tf_op jit(solution)/shard_map/dot_general | solution.py:532
  185.2 6.3 %copy.19 = bf16[4096,512]{0,1:T(8,128)(2,1)} copy(bf16[4096,512]{1,0:T(8,128)(2,1)} %bitcast.54) | data formatting | bytes 8388608 | tf_op jit(solution)/shard_map/reshape | solution.py:528
  191.5 0.0 copy-start
  191.5 2.2 copy-done
  193.7 0.0 copy-start.5
  193.7 36.5 %last.1 = bf16[16,4096]{1,0:T(8,128)(2,1)S(1)} custom-call(bf16[4,2,4,16,4096]{4,3,2,1,0:T(8,128)(2,1)S(1)} %bitcast.43, bf16[16,4096]{1,0:T(8,128)(2,1)S(1)} %get-tuple-element.20.middle), custom_call_target="tpu_custom_call" | custom-call | tf_op jit(solution)/shard_map/last/pallas_call | solution.py:487
  230.2 0.7 copy.26
  230.8 0.0 copy-done.5
  230.8 2.0 copy.27
  (3 shorter events, 0.0 us)
Async XLA Ops:
  0.7 3.5 %copy-start.4 = (bf16[512,4096]{1,0:T(8,128)(2,1)S(1)}, bf16[512,4096]{1,0:T(8,128)(2,1)}, u32[]{:S(2)}) copy-start(bf16[512,4096]{1,0:T(8,128)(2,1)} %hidden.1) | copy-start | bytes 12582916
  0.7 4.7 %copy-start.1 = (f32[32,3,4096]{2,0,1:T(8,128)S(1)}, f32[32,3,4096]{2,0,1:T(8,128)}, u32[]{:S(2)}) copy-start(f32[32,3,4096]{2,0,1:T(8,128)} %param.12) | copy-start | bytes 4718596
  0.7 4.7 %copy-start.2 = (f32[4096,32]{0,1:T(8,128)S(1)}, f32[4096,32]{0,1:T(8,128)}, u32[]{:S(2)}) copy-start(f32[4096,32]{0,1:T(8,128)} %param.13) | copy-start | bytes 1572868
  54.7 3.6 %copy-start.9 = (f32[4096]{0:T(1024)S(1)}, f32[4096]{0:T(1024)}, u32[]{:S(2)}) copy-start(f32[4096]{0:T(1024)} %param.10) | copy-start | bytes 49156
  58.3 2.0 copy-start.7
  58.4 5.6 %copy-start.10 = (s32[512]{0:T(512)S(1)}, s32[512]{0:T(512)}, u32[]{:S(2)}) copy-start(s32[512]{0:T(512)} %param.9) | copy-start | bytes 6148
  60.4 0.8 copy-start.8
  65.5 1.0 copy-start.6
  65.5 6.1 %copy-start.3 = (f32[4096]{0:T(1024)S(1)}, f32[4096]{0:T(1024)}, u32[]{:S(2)}) copy-start(f32[4096]{0:T(1024)} %param.11) | copy-start | bytes 49156
  191.5 2.2 copy-start
  193.7 37.2 %copy-start.5 = (bf16[4,4,2,128,512]{4,3,2,1,0:T(8,128)(2,1)S(1)}, bf16[4,4,2,128,512]{4,3,2,1,0:T(8,128)(2,1)}, u32[]{:S(2)}) copy-start(bf16[4,4,2,128,512]{4,3,2,1,0:T(8,128)(2,1)} %get-tuple-element.18) | copy-start | bytes 12582916

commit v2 on v0

v2 whole, which is shorter than its diff:
```python
import math

import jax
import jax.numpy as jnp
from jax import lax
from jax.experimental import pallas as pl
from jax.experimental.pallas import tpu as pltpu
from jax.sharding import PartitionSpec as P

D = 4096
HD = 128
EPSILON = 1e-05
MESH = pl.DeviceIdType.MESH
BF16 = jnp.bfloat16
F32 = jnp.float32


class Place:
    def __init__(self):
        self.dp = lax.axis_index("dp")
        self.t = lax.axis_index("tensor")
        self.zl = self.dp // 2
        self.core = self.dp % 2
        self.x = self.t // 8
        self.zh = (self.t // 4) % 2
        self.y = self.t % 4
        self.z_pair = (1 - self.zl) * 2 + self.core
        self.core_pair = self.zl * 2 + (1 - self.core)

    def near(self, axis, delta):
        if axis == "x":
            return (self.dp, ((self.x + delta) % 4) * 8 + self.zh * 4 + self.y)
        return (self.dp, self.x * 8 + self.zh * 4 + (self.y + delta) % 4)

    def across(self):
        return (self.dp, self.x * 8 + (1 - self.zh) * 4 + self.y)


def remote(src, dst, send_sem, recv_sem, device):
    return pltpu.make_async_remote_copy(
        src_ref=src,
        dst_ref=dst,
        send_sem=send_sem,
        recv_sem=recv_sem,
        device_id=device,
        device_id_type=MESH,
    )


def greet(barrier, device):
    pl.semaphore_signal(barrier, inc=1, device_id=device, device_id_type=MESH)


HALF = 2048


def reduce_rows(me, share, bufs, sems, between):
    ra, acc_a, rb, acc_b, kept, last, last_half, rc = bufs
    sa, qa, sb, qb, sc, qc = sems
    axes = (("x", "y"), ("y", "x"))

    def chunk_a(f, q, h):
        if f == 0:
            return share.at[q, h, :, :, pl.ds(0, HALF)]
        return share.at[:, h, q, :, pl.ds(HALF, HALF)]

    def chunk_b(f, q, h):
        return kept.at[f, q, h]

    def position(axis):
        return me.x if axis == "x" else me.y

    def stage(level, chunk, recv, acc, s_sem, r_sem, store):
        started = []
        plan = []
        for f in range(2):
            axis = axes[f][level]
            p = position(axis)
            far = (p + 2) % 4
            for way in range(2):
                delta = 1 - 2 * way
                near = (p + delta) % 4
                device = me.near(axis, delta)
                first = remote(
                    chunk(f, far, way), recv.at[f, way, 0], s_sem.at[f, way, 0], r_sem.at[f, way, 0], device
                )
                plain = remote(
                    chunk(f, near, 1 - way), recv.at[f, way, 1], s_sem.at[f, way, 1], r_sem.at[f, way, 1], device
                )
                summed = remote(
                    acc.at[f, way], recv.at[f, way, 2], s_sem.at[f, way, 2], r_sem.at[f, way, 2], device
                )
                plan.append((f, way, near, first, plain, summed))
        for f, way, near, first, plain, summed in plan:
            first.start()
        for f, way, near, first, plain, summed in plan:
            plain.start()
        for f, way, near, first, plain, summed in plan:
            first.wait_recv()
            acc[f, way] = (chunk(f, near, way)[...].astype(F32) + recv[f, way, 0].astype(F32)).astype(BF16)
            summed.start()
        for f in range(2):
            p = position(axes[f][level])
            both = [entry for entry in plan if entry[0] == f]
            for h in range(2):
                both[1 - h][4].wait_recv()
                both[h][5].wait_recv()
                total = (
                    chunk(f, p, h)[...].astype(F32)
                    + recv[f, h, 2].astype(F32)
                    + recv[f, 1 - h, 1].astype(F32)
                )
                store(f, h, total)
        for f, way, near, first, plain, summed in plan:
            first.wait_send()
            plain.wait_send()
            summed.wait_send()

    def store_a(f, h, total):
        kept[f, :, h] = total.astype(BF16)

    def store_b(f, h, total):
        last[f, h] = total
        last_half[f, h] = total.astype(BF16)

    stage(0, chunk_a, ra, acc_a, sa, qa, store_a)
    between()
    stage(1, chunk_b, rb, acc_b, sb, qb, store_b)
    swaps = [
        remote(last_half.at[f, 1 - me.zh], rc.at[f], sc.at[f], qc.at[f], me.across()) for f in range(2)
    ]
    for swap in swaps:
        swap.start()
    sums = []
    for f, swap in enumerate(swaps):
        swap.wait_recv()
        sums.append(last[f, me.zh] + rc[f].astype(F32))
    for swap in swaps:
        swap.wait_send()
    return sums


def reduce_scratch():
    dma = pltpu.SemaphoreType.DMA
    bufs = [
        pltpu.VMEM((2, 2, 3, 4, 16, HALF), BF16),
        pltpu.VMEM((2, 2, 4, 16, HALF), BF16),
        pltpu.VMEM((2, 2, 3, 16, HALF), BF16),
        pltpu.VMEM((2, 2, 16, HALF), BF16),
        pltpu.VMEM((2, 4, 2, 16, HALF), BF16),
        pltpu.VMEM((2, 2, 16, HALF), F32),
        pltpu.VMEM((2, 2, 16, HALF), BF16),
        pltpu.VMEM((2, 16, HALF), BF16),
    ]
    sems = [dma((2, 2, 3)), dma((2, 2, 3)), dma((2, 2, 3)), dma((2, 2, 3)), dma((2,)), dma((2,))]
    return bufs, sems


class Relay:
    def __init__(self, me, source, wide, stage, sems):
        self.me, self.source, self.wide, self.stage = me, source, wide, stage
        self.s, self.own, self.r, self.zs, self.zr, self.cs, self.cr, self.ps, self.pr = sems

    def holder(self, step):
        me = self.me
        other = (me.t + step) % 32
        apart = (me.zh + (other // 4) % 2) % 2
        return other, apart, ((me.zl + apart) % 2) * 2 + me.core

    def group(self, slot, flip_z, flip_c):
        me = self.me
        apart = slot // 4
        zl = (me.zl + apart + flip_z) % 2
        core = (me.core + flip_c) % 2
        return (zl * 2 + core) * 8 + (slot % 4) * 2 + (me.zh + apart) % 2

    def at(self, group, rows=None):
        lead = (slice(None),) * (len(self.stage.shape) - 3)
        if rows is None:
            return self.stage.at[lead + (group,)]
        return self.stage.at[lead + (group, rows)]

    def cut(self, other):
        lead = (slice(None),) * (len(self.source.shape) - 1)
        return self.source.at[lead + (pl.ds(pl.multiple_of(other * self.wide, self.wide), self.wide),)]

    def own_piece(self):
        me = self.me
        mine = me.dp * 8 + me.x * 2 + me.zh
        return self.at(mine, pl.ds(pl.multiple_of(me.y * 32, 32), 32))

    def send(self):
        me = self.me

        def body(step, carry):
            other, apart, group = self.holder(step)
            remote(
                self.cut(other), self.own_piece(), self.s, self.r.at[apart * 4 + me.x], (group, other)
            ).start()
            return carry

        lax.fori_loop(1, 32, body, 0)
        pltpu.make_async_copy(self.cut(me.t), self.own_piece(), self.own).start()

    def settle(self):
        pltpu.make_async_copy(self.cut(self.me.t), self.own_piece(), self.own).wait()

    def wait_slot(self, slot):
        me = self.me
        group = self.group(slot, 0, 0)

        def got(count):
            ref = self.at(group, pl.ds(0, count))
            remote(ref, ref, self.s, self.r.at[slot], (me.core_pair, me.t)).wait_recv()

        @pl.when(slot != me.x)
        def _():
            got(128)

        @pl.when(slot == me.x)
        def _():
            got(96)

    def to_z(self, slot):
        ref = self.at(self.group(slot, 0, 0))
        return remote(ref, ref, self.zs.at[slot], self.zr.at[slot], (self.me.z_pair, self.me.t))

    def to_core(self, slot):
        ref = self.at(self.group(slot, 0, 0))
        return remote(ref, ref, self.cs.at[slot], self.cr.at[slot], (self.me.core_pair, self.me.t))

    def pass_on(self, slot):
        ref = self.at(self.group(slot, 1, 0))
        return remote(ref, ref, self.ps.at[slot], self.pr.at[slot], (self.me.core_pair, self.me.t))

    def got(self, slot, flip_z, flip_c, sem):
        ref = self.at(self.group(slot, flip_z, flip_c))
        remote(ref, ref, self.s, sem, (self.me.core_pair, self.me.t)).wait_recv()

    def forward(self, first, last):
        def body(slot, carry):
            self.wait_slot(slot)
            self.to_z(slot).start()
            self.to_core(slot).start()
            return carry

        lax.fori_loop(first, last, body, 0)

    def relay_on(self, first, last):
        def body(slot, carry):
            self.got(slot, 1, 0, self.zr.at[slot])
            self.pass_on(slot).start()
            return carry

        lax.fori_loop(first, last, body, 0)

    def complete(self):
        def body(slot, carry):
            self.got(slot, 0, 1, self.cr.at[slot])
            self.got(slot, 1, 1, self.pr.at[slot])
            return carry

        lax.fori_loop(0, 8, body, 0)

    def drain(self):
        def body(slot, carry):
            self.to_z(slot).wait_send()
            self.to_core(slot).wait_send()
            self.pass_on(slot).wait_send()
            return carry

        lax.fori_loop(0, 8, body, 0)
        lead = (slice(None),) * (len(self.source.shape) - 1)
        sent = self.source.at[lead + (pl.ds(0, 31 * self.wide),)]
        remote(sent, sent, self.s, self.s, (self.me.core_pair, self.me.t)).wait_send()


def norm_rows(values, gain):
    center = values - jnp.mean(values, axis=-1, keepdims=True)
    spread = jnp.mean(center * center, axis=-1, keepdims=True)
    return (center * lax.rsqrt(spread + EPSILON) * gain).astype(BF16)


def gather_rows(me, field, view, axes, s_sem, r_sem, between):
    plan = []
    for f in range(2):
        axis = axes[f]
        p = me.x if axis == "x" else me.y
        for way in range(2):
            delta = 1 - 2 * way
            device = me.near(axis, delta)
            unit = view(f, p, None)
            came = view(f, (p + 4 - delta) % 4, way)
            plan.append(
                (
                    remote(unit, unit, s_sem.at[f, way, 0], r_sem.at[f, way, 0], device),
                    remote(came, came, s_sem.at[f, way, 1], r_sem.at[f, way, 1], device),
                )
            )
    for whole, half in plan:
        whole.start()
    between()
    for whole, half in plan:
        whole.wait_recv()
        half.start()
    for whole, half in plan:
        half.wait_recv()
    for whole, half in plan:
        whole.wait_send()
        half.wait_send()


def attend(queries, keys, values, seg_col, seg_row, slope, context):
    scale = 1.0 / math.sqrt(HD)
    for block in range(4):
        rows = pl.ds(block * 128, 128)
        reach = (block + 1) * 128
        cols = pl.ds(0, reach)
        scores = (
            lax.dot_general(
                queries[rows, :], keys[cols, :], (((1,), (1,)), ((), ())), preferred_element_type=F32
            )
            * scale
        )
        n = lax.broadcasted_iota(jnp.int32, (128, reach), 0) + block * 128
        p = lax.broadcasted_iota(jnp.int32, (128, reach), 1)
        scores = scores - slope * (n - p).astype(F32)
        allowed = (seg_col[rows, :] == seg_row[:, cols]) & (p <= n)
        scores = jnp.where(allowed, scores, -jnp.inf)
        highest = jnp.max(scores, axis=-1, keepdims=True)
        raised = jnp.exp(scores - highest)
        weights = (raised / jnp.sum(raised, axis=-1, keepdims=True)).astype(BF16)
        context[rows, :] = jnp.dot(weights, values[cols, :], preferred_element_type=F32).astype(BF16)


def layer_kernel(*refs):
    (hidden, seg_col, seg_row, slope, gain_one, gain_two, q_in, o_in, u_in, w_in) = refs[:10]
    (new_hidden, key_out, value_out, qkv_out, out_out, up_out, down_out) = refs[10:17]
    rest = refs[17:]
    (q_f, o_f, u_f, w_f, h_v, sq, su, sw, qo, up, down, normed, field, share, acc, q_v, k_v, v_v, ctx, act, middle, result) = rest[:22]
    in_sem, out_sem = rest[22:24]
    relay_sems = [rest[24 + 9 * k : 33 + 9 * k] for k in range(3)]
    rest = rest[51:]
    bufs_one, sems_one, bufs_two, sems_two = rest[:8], rest[8:14], rest[14:22], rest[22:28]
    a_s, a_r, b_s, b_r, x_s, x_r = rest[28:]
    me = Place()

    loads = [
        pltpu.make_async_copy(src, dst, in_sem.at[k])
        for k, (src, dst) in enumerate(
            ((q_in, q_f), (o_in, o_f), (u_in, u_f), (w_in, w_f), (hidden, h_v))
        )
    ]
    for load in loads:
        load.start()
    r_q = Relay(me, sq, 128, qo, relay_sems[0])
    r_u = Relay(me, su, 512, up, relay_sems[1])
    r_d = Relay(me, sw, 512, down, relay_sems[2])

    barrier = pltpu.get_barrier_semaphore()

    def hello(step, carry):
        other, _, group = r_q.holder(step)
        greet(barrier, (group, other))
        return carry

    lax.fori_loop(1, 32, hello, 0)
    greet(barrier, (me.z_pair, me.t))
    greet(barrier, (me.core_pair, me.t))
    greet(barrier, me.across())
    loads[0].wait()
    loads[1].wait()
    sq[0:3] = q_f[...].astype(BF16)
    sq[3] = o_f[...].astype(BF16)
    pl.semaphore_wait(barrier, 34)
    r_q.send()

    loads[4].wait()
    r_q.settle()

    def opening(slot, carry):
        @pl.loop(0, 2)
        def _(part):
            rows = pl.ds(pl.multiple_of(slot * 64 + part * 32, 32), 32)
            normed[rows, :] = norm_rows(h_v[rows, :].astype(F32), gain_one[...])

        r_q.wait_slot(slot)
        r_q.to_z(slot).start()
        r_q.to_core(slot).start()
        return carry

    lax.fori_loop(0, 8, opening, 0)

    loads[2].wait()
    loads[3].wait()

    @pl.loop(0, 4)
    def _(part):
        cols = pl.ds(pl.multiple_of(part * 4096, 4096), 4096)
        su[:, cols] = u_f[:, cols].astype(BF16)

    r_u.send()

    @pl.loop(0, 4)
    def _(part):
        cols = pl.ds(pl.multiple_of(part * 4096, 4096), 4096)
        sw[:, cols] = w_f[:, cols].astype(BF16)

    r_d.send()
    r_q.relay_on(0, 8)
    r_u.settle()
    r_d.settle()
    r_u.forward(0, 8)
    r_q.complete()
    save_q = pltpu.make_async_copy(qo.at[pl.ds(0, 3)], qkv_out, out_sem.at[0])
    save_o = pltpu.make_async_copy(qo.at[3], out_out, out_sem.at[1])
    save_q.start()
    save_o.start()

    acc_q = acc.at[:, pl.ds(0, 384)]
    for part in range(8):
        cols = pl.ds(part * 512, 512)
        block = jnp.concatenate(
            [qo[k, part * 4 : part * 4 + 4].reshape(512, 128) for k in range(3)], axis=1
        )
        product = jnp.dot(normed[:, cols], block, preferred_element_type=F32)
        if part == 0:
            acc_q[...] = product
        else:
            acc_q[...] += product
    q_v[...] = acc[:, 0:128].astype(BF16)
    k_v[...] = acc[:, 128:256].astype(BF16)
    v_v[...] = acc[:, 256:384].astype(BF16)
    save_k = pltpu.make_async_copy(k_v, key_out, out_sem.at[2])
    save_v = pltpu.make_async_copy(v_v, value_out, out_sem.at[3])
    save_k.start()
    save_v.start()
    attend(q_v, k_v, v_v, seg_col, seg_row, slope[0:1, 0:1], ctx)

    @pl.loop(0, 8)
    def _(part):
        block = qo[3, pl.ds(part * 4, 4)].reshape(512, 128)
        product = lax.dot_general(
            ctx[...], block, (((1,), (1,)), ((), ())), preferred_element_type=F32
        ).astype(BF16)
        cols = pl.ds(pl.multiple_of(part * 512, 512), 512)
        share[:, :, :, :, cols] = product.reshape(4, 2, 4, 16, 512)

    def after_first():
        r_u.relay_on(0, 8)
        r_d.forward(0, 4)

    left, right = reduce_rows(me, share, bufs_one, sems_one, after_first)
    own_rows = pl.ds(pl.multiple_of(me.t * 16, 16), 16)
    middle[:, :HALF] = (h_v[own_rows, :HALF].astype(F32) + left).astype(BF16)
    middle[:, HALF:] = (h_v[own_rows, HALF:].astype(F32) + right).astype(BF16)
    field[me.x, me.zh, me.y] = norm_rows(middle[...].astype(F32), gain_two[...])

    spot = field.at[me.x, me.zh, me.y]
    swap = remote(spot, spot, x_s, x_r, me.across())
    swap.start()
    swap.wait_recv()
    swap.wait_send()

    def view_b(f, q, h):
        cols = pl.ds(f * HALF, HALF)
        lane = slice(None) if h is None else h
        if f == 0:
            return field.at[me.x, lane, q, :, cols]
        return field.at[q, lane, me.y, :, cols]

    def view_a(f, q, h):
        cols = pl.ds(f * HALF, HALF)
        lane = slice(None) if h is None else h
        if f == 0:
            return field.at[q, lane, :, :, cols]
        return field.at[:, lane, q, :, cols]

    def rest_of_down():
        r_d.forward(4, 8)
        r_d.relay_on(0, 4)

    gather_rows(me, field, view_b, ("y", "x"), b_s, b_r, rest_of_down)
    gather_rows(me, field, view_a, ("x", "y"), a_s, a_r, lambda: None)
    r_u.complete()
    save_u = pltpu.make_async_copy(up, up_out, out_sem.at[4])
    save_u.start()
    r_d.relay_on(4, 8)

    for part in range(8):
        rows = field[:, :, :, :, part * 512 : part * 512 + 512].reshape(512, 512)
        block = up[part * 4 : part * 4 + 4].reshape(512, 512)
        product = jnp.dot(rows, block, preferred_element_type=F32)
        if part == 0:
            acc[...] = product
        else:
            acc[...] += product

    @pl.loop(0, 8)
    def _(part):
        rows = pl.ds(pl.multiple_of(part * 64, 64), 64)
        values = acc[rows, :]
        act[rows, :] = (0.5 * values * (1.0 + lax.erf(values * math.sqrt(0.5)))).astype(BF16)

    r_d.complete()
    save_d = pltpu.make_async_copy(down, down_out, out_sem.at[5])
    save_d.start()

    @pl.loop(0, 8)
    def _(part):
        block = down[pl.ds(part * 4, 4)].reshape(512, 512)
        product = lax.dot_general(
            act[...], block, (((1,), (1,)), ((), ())), preferred_element_type=F32
        ).astype(BF16)
        cols = pl.ds(pl.multiple_of(part * 512, 512), 512)
        share[:, :, :, :, cols] = product.reshape(4, 2, 4, 16, 512)

    left, right = reduce_rows(me, share, bufs_two, sems_two, lambda: None)
    result[:, :HALF] = (middle[:, :HALF].astype(F32) + left).astype(BF16)
    result[:, HALF:] = (middle[:, HALF:].astype(F32) + right).astype(BF16)
    save_n = pltpu.make_async_copy(result, new_hidden, out_sem.at[6])
    save_n.start()
    for relay in (r_q, r_u, r_d):
        relay.drain()
    for save in (save_q, save_o, save_k, save_v, save_u, save_d, save_n):
        save.wait()


def layer(hidden, seg, slope, gain_one, gain_two, qkv, out, up, down):
    any_spec = pl.BlockSpec(memory_space=pl.ANY)
    vmem = pl.BlockSpec(memory_space=pltpu.VMEM)
    dma = pltpu.SemaphoreType.DMA
    bufs_one, sems_one = reduce_scratch()
    bufs_two, sems_two = reduce_scratch()
    relay_sems = [dma(()), dma(())] + [dma((8,))] * 7
    return pl.pallas_call(
        layer_kernel,
        out_shape=(
            jax.ShapeDtypeStruct((16, D), BF16),
            jax.ShapeDtypeStruct((512, HD), BF16),
            jax.ShapeDtypeStruct((512, HD), BF16),
            jax.ShapeDtypeStruct((3, 32, 128, HD), BF16),
            jax.ShapeDtypeStruct((32, 128, HD), BF16),
            jax.ShapeDtypeStruct((32, 128, 512), BF16),
            jax.ShapeDtypeStruct((32, 128, 512), BF16),
        ),
        in_specs=[any_spec, vmem, vmem, vmem, vmem, vmem] + [any_spec] * 4,
        out_specs=[any_spec] * 7,
        scratch_shapes=[
            pltpu.VMEM((3, 32, 4096), F32),
            pltpu.VMEM((32, 4096), F32),
            pltpu.VMEM((32, 16384), F32),
            pltpu.VMEM((32, 16384), F32),
            pltpu.VMEM((512, D), BF16),
            pltpu.VMEM((4, 32, 4096), BF16),
            pltpu.VMEM((32, 16384), BF16),
            pltpu.VMEM((32, 16384), BF16),
            pltpu.VMEM((4, 32, 128, 128), BF16),
            pltpu.VMEM((32, 128, 512), BF16),
            pltpu.VMEM((32, 128, 512), BF16),
            pltpu.VMEM((512, D), BF16),
            pltpu.VMEM((4, 2, 4, 16, D), BF16),
            pltpu.VMEM((4, 2, 4, 16, D), BF16),
            pltpu.VMEM((512, 512), F32),
            pltpu.VMEM((512, HD), BF16),
            pltpu.VMEM((512, HD), BF16),
            pltpu.VMEM((512, HD), BF16),
            pltpu.VMEM((512, HD), BF16),
            pltpu.VMEM((512, 512), BF16),
            pltpu.VMEM((16, D), BF16),
            pltpu.VMEM((16, D), BF16),
            dma((5,)),
            dma((7,)),
        ]
        + relay_sems * 3
        + bufs_one
        + sems_one
        + bufs_two
        + sems_two
        + [dma((2, 2, 2))] * 4
        + [dma(()), dma(())],
        compiler_params=pltpu.CompilerParams(
            collective_id=0, has_side_effects=True, vmem_limit_bytes=62 << 20
        ),
        name="layer",
    )(hidden, seg.reshape(512, 1), seg.reshape(1, 512), slope, gain_one, gain_two, qkv, out, up, down)


def shards(
    hidden, segment_ids, first_gain, second_gain, qkv_master, out_master, up_master, down_master
):
    slope = jnp.exp2(-8.0 * (lax.axis_index("tensor").astype(F32) + 1.0) / (D // HD))
    new_hidden, keys, values, qkv, out_t, up, down_t = layer(
        hidden,
        segment_ids,
        jnp.full((1, 128), slope, F32),
        first_gain.reshape(1, D),
        second_gain.reshape(1, D),
        qkv_master.transpose(1, 0, 2),
        out_master.T,
        up_master,
        down_master.T,
    )
    return (
        new_hidden,
        keys,
        values,
        qkv.reshape(3, D, HD).transpose(1, 0, 2),
        out_t.reshape(D, HD).T,
        up.reshape(D, 512),
        down_t.reshape(D, 512).T,
    )


def solution(mesh):
    in_specs = (
        P("dp", None),
        P("dp"),
        P(),
        P(),
        P(("dp", "tensor"), None, None),
        P(None, ("dp", "tensor")),
        P(("dp", "tensor"), None),
        P(None, ("dp", "tensor")),
    )
    out_specs = (
        P(("dp", "tensor"), None),
        P("dp", "tensor"),
        P("dp", "tensor"),
        P(None, None, "tensor"),
        P("tensor", None),
        P(None, "tensor"),
        P("tensor", None),
    )
    return jax.shard_map(shards, mesh=mesh, in_specs=in_specs, out_specs=out_specs, check_vma=False)
```

time: 821 us -> 184 us (0.22)
  waiting for transfers between devices: 477 us -> 0 us
  Pallas kernels: 0 us -> 167 us
  other arithmetic: 106 us -> 0 us
  blocking collectives: 92.2 us -> 0 us
  local copies, waits for them, and re-layouts: 88 us -> 16.5 us
  matrix products: 21.3 us -> 0 us
  starting transfers between devices: 20.5 us -> 0 us
  between operations: 14.3 us -> 0.7 us
    reduce_scatter x2 -> x0, waiting for transfers between devices: 347 us -> none  [the longest x1 182 us: shards(): lax.psum_scatter(jnp.dot(activated, down_block, preferred_element_type=jn...]
    pallas_call x0 -> x1, Pallas kernels: none -> 167 us  [layer(): pl.pallas_call(layer_kernel, out_shape=(jax.ShapeDtypeStruct((16, D), BF1...]
    all_to_all x2 -> x0, blocking collectives: 92.2 us -> none  [the longest x1 65.8 us: shards(): lax.all_to_all(up_rows, 'tensor', split_axis=2, concat_axis=0, tiled=True)]
    unnamed x1 -> x0, other arithmetic: 90.7 us -> none
    all_gather x5 -> x0, waiting for transfers between devices: 72.1 us -> none  [the longest x1 41.2 us: shards(): lax.all_gather(up_half, 'dp', axis=0, tiled=True)]
    all_to_all x2 -> x0, waiting for transfers between devices: 57.7 us -> none  [the longest x1 57.7 us: shards(): lax.all_to_all(qkv_rows, 'tensor', split_axis=2, concat_axis=0, tiled=True)]
    unnamed x28 -> x15, local copies, waits for them, and re-layouts: 43.5 us -> 5.66 us
    all_gather x2 -> x0, local copies, waits for them, and re-layouts: 25 us -> none  [the longest x1 17.8 us: shards(): lax.all_gather(up_half, 'dp', axis=0, tiled=True)]
  transfers between devices with their start and end apart: 9 -> 0, of which waited for: 5 -> 0; matrix products, arithmetic and copies ran while one was open for 23% -> 0% of each run, Pallas kernels for 0% -> 0%
where the time goes in v2:
time: 184 us
  Pallas kernels  167 us (91%)
  local copies, waits for them, and re-layouts  16.5 us (9%)
    pallas_call x1, Pallas kernels, layer(): pl.pallas_call(layer_kernel, out_shape=(jax.ShapeDtypeStruct((16, D), BF1...  167 us
    reshape x1, local copies, waits for them, and re-layouts, shards(): down_t.reshape(D, 512)  6.48 us
    unnamed x15, local copies, waits for them, and re-layouts  5.66 us

profile of v2, /device:TPU:0, one launch (start us, length us, event | category | flops | bytes accessed | tf_op | source)
XLA Modules:
  0.0 183.8 jit_solution(1121504140140606877)
XLA Ops:
  0.7 0.5 broadcast_in_dim.3.refs_3_
  1.2 1.5 copy.17.refs_1_
  2.7 166.7 %layer.1 = (bf16[16,4096]{1,0:T(8,128)(2,1)}, bf16[512,128]{1,0:T(8,128)(2,1)}, bf16[512,128]{1,0:T(8,128)(2,1)}, bf16[3,32,128,128]{3,2,1,0:T(8,128)(2,1)}, bf1...) custom-call(bf16[512,4096]{1,0:T(8,128)(2,1)} %refs_0_.1, ...), custom_call_target="tpu_custom_call" | custom-call | tf_op jit(solution)/shard_map/layer/pallas_call | solution.py:536
  169.4 2.3 %copy.18 = bf16[4096,128]{0,1:T(8,128)(2,1)} copy(bf16[4096,128]{1,0:T(8,128)(2,1)} %bitcast.22) | data formatting | bytes 2097152 | tf_op jit(solution)/shard_map/reshape | solution.py:609
  171.7 0.0 copy-start.4
  171.7 0.0 copy-start.3
  171.7 0.0 copy-start.2
  171.7 0.0 copy-start.1
  171.7 6.5 %copy.19 = bf16[4096,512]{0,1:T(8,128)(2,1)} copy(bf16[4096,512]{1,0:T(8,128)(2,1)} %bitcast.17) | data formatting | bytes 8388608 | tf_op jit(solution)/shard_map/reshape | solution.py:611
  178.1 0.0 copy-start
  178.1 0.0 copy-done.4
  178.1 0.7 copy.25
  178.8 0.0 copy-done.3
  178.8 0.7 copy.26
  179.5 0.0 copy-done.2
  179.5 0.7 copy.27
  180.1 0.0 copy-done.1
  180.1 1.7 copy.28
  181.8 0.0 copy-done
  181.8 2.0 %copy.29 = bf16[4096,512]{1,0:T(8,128)(2,1)} copy(bf16[4096,512]{1,0:T(8,128)(2,1)S(1)} %bitcast.16) | data formatting | bytes 8388608
Async XLA Ops:
  171.7 6.5 %copy-start.4 = (bf16[16,4096]{1,0:T(8,128)(2,1)S(1)}, bf16[16,4096]{1,0:T(8,128)(2,1)}, u32[]{:S(2)}) copy-start(bf16[16,4096]{1,0:T(8,128)(2,1)} %get-tuple-element.28) | copy-start | bytes 393220
  171.7 7.2 %copy-start.3 = (bf16[512,128]{1,0:T(8,128)(2,1)S(1)}, bf16[512,128]{1,0:T(8,128)(2,1)}, u32[]{:S(2)}) copy-start(bf16[512,128]{1,0:T(8,128)(2,1)} %get-tuple-element.29) | copy-start | bytes 393220
  171.7 7.8 %copy-start.2 = (bf16[512,128]{1,0:T(8,128)(2,1)S(1)}, bf16[512,128]{1,0:T(8,128)(2,1)}, u32[]{:S(2)}) copy-start(bf16[512,128]{1,0:T(8,128)(2,1)} %get-tuple-element.30) | copy-start | bytes 393220
  171.7 8.5 %copy-start.1 = (bf16[3,32,128,128]{3,2,1,0:T(8,128)(2,1)S(1)}, bf16[3,32,128,128]{3,2,1,0:T(8,128)(2,1)}, u32[]{:S(2)}) copy-start(bf16[3,32,128,128]{3,2,1,0:T(8,128)(2,1)} %get-tuple-element.17) | copy-start | bytes 9437188
  178.1 3.6 %copy-start = (bf16[32,128,512]{2,1,0:T(8,128)(2,1)S(1)}, bf16[32,128,512]{2,1,0:T(8,128)(2,1)}, u32[]{:S(2)}) copy-start(bf16[32,128,512]{2,1,0:T(8,128)(2,1)} %get-tuple-element.19) | copy-start | bytes 12582916

commit v3 on v2

v3 whole, which is shorter than its diff:
```python
import math

import jax
import jax.numpy as jnp
from jax import lax
from jax.experimental import pallas as pl
from jax.experimental.pallas import tpu as pltpu
from jax.sharding import PartitionSpec as P

D = 4096
HD = 128
EPSILON = 1e-05
MESH = pl.DeviceIdType.MESH
BF16 = jnp.bfloat16
F32 = jnp.float32


class Place:
    def __init__(self):
        self.dp = lax.axis_index("dp")
        self.t = lax.axis_index("tensor")
        self.zl = self.dp // 2
        self.core = self.dp % 2
        self.x = self.t // 8
        self.zh = (self.t // 4) % 2
        self.y = self.t % 4
        self.z_pair = (1 - self.zl) * 2 + self.core
        self.core_pair = self.zl * 2 + (1 - self.core)

    def near(self, axis, delta):
        if axis == "x":
            return (self.dp, ((self.x + delta) % 4) * 8 + self.zh * 4 + self.y)
        return (self.dp, self.x * 8 + self.zh * 4 + (self.y + delta) % 4)

    def across(self):
        return (self.dp, self.x * 8 + (1 - self.zh) * 4 + self.y)


def remote(src, dst, send_sem, recv_sem, device):
    return pltpu.make_async_remote_copy(
        src_ref=src,
        dst_ref=dst,
        send_sem=send_sem,
        recv_sem=recv_sem,
        device_id=device,
        device_id_type=MESH,
    )


def greet(barrier, device):
    pl.semaphore_signal(barrier, inc=1, device_id=device, device_id_type=MESH)


HALF = 2048
PART = 1024


def reduce_rows(me, share, bufs, sems, while_first, while_second, pump=lambda count: None):
    ra, acc_a, rb, acc_b, kept, last, last_half, rc = bufs
    sa, qa, sb, qb, sc, qc = sems
    axes = (("x", "y"), ("y", "x"))

    def chunk_a(f, s, q, h):
        cols = pl.ds(f * HALF + s * PART, PART)
        if f == 0:
            return share.at[q, h, :, :, cols]
        return share.at[:, h, q, :, cols]

    def chunk_b(f, s, q, h):
        return kept.at[f, s, q, h]

    def position(f, level):
        return me.x if axes[f][level] == "x" else me.y

    class Ring:
        def __init__(self, level, s, chunk, recv, acc, s_sem, r_sem):
            self.level, self.s, self.chunk, self.recv, self.acc = level, s, chunk, recv, acc
            self.plan = []
            for f in range(2):
                p = position(f, level)
                far = (p + 2) % 4
                for way in range(2):
                    delta = 1 - 2 * way
                    near = (p + delta) % 4
                    device = me.near(axes[f][level], delta)
                    copies = [
                        remote(src, recv.at[f, s, way, k], s_sem.at[f, s, way, k], r_sem.at[f, s, way, k], device)
                        for k, src in enumerate(
                            (chunk(f, s, far, way), chunk(f, s, near, 1 - way), acc.at[f, s, way])
                        )
                    ]
                    self.plan.append((f, way, near, copies))

        def start(self, k):
            for f, way, near, copies in self.plan:
                copies[k].start()

        def accumulate(self):
            s = self.s
            for f, way, near, copies in self.plan:
                copies[0].wait_recv()
                self.acc[f, s, way] = (
                    self.chunk(f, s, near, way)[...].astype(F32) + self.recv[f, s, way, 0].astype(F32)
                ).astype(BF16)
                copies[2].start()

        def finalize(self, store):
            s = self.s
            for f in range(2):
                p = position(f, self.level)
                both = [entry[3] for entry in self.plan if entry[0] == f]
                for h in range(2):
                    both[1 - h][1].wait_recv()
                    both[h][2].wait_recv()
                    total = (
                        self.chunk(f, s, p, h)[...].astype(F32)
                        + self.recv[f, s, h, 2].astype(F32)
                        + self.recv[f, s, 1 - h, 1].astype(F32)
                    )
                    store(f, s, h, total)

        def drain(self):
            for f, way, near, copies in self.plan:
                for copy in copies:
                    copy.wait_send()

    def store_a(f, s, h, total):
        kept[f, s, :, h] = total.astype(BF16)

    def store_b(f, s, h, total):
        last[f, s, h] = total
        last_half[f, s, h] = total.astype(BF16)

    first = [Ring(0, s, chunk_a, ra, acc_a, sa, qa) for s in range(2)]
    second = [Ring(1, s, chunk_b, rb, acc_b, sb, qb) for s in range(2)]
    swaps = [
        [remote(last_half.at[f, s, 1 - me.zh], rc.at[f, s], sc.at[f, s], qc.at[f, s], me.across()) for f in range(2)]
        for s in range(2)
    ]
    first[0].start(0)
    first[0].start(1)
    first[1].start(0)
    pump(1)
    while_first()
    pump(1)
    first[0].accumulate()
    first[1].start(1)
    pump(1)
    first[1].accumulate()
    pump(1)
    first[0].finalize(store_a)
    second[0].start(0)
    second[0].start(1)
    pump(1)
    while_second()
    second[0].accumulate()
    pump(1)
    first[1].finalize(store_a)
    second[1].start(0)
    second[1].start(1)
    second[0].finalize(store_b)
    for swap in swaps[0]:
        swap.start()
    second[1].accumulate()
    second[1].finalize(store_b)
    for swap in swaps[1]:
        swap.start()
    sums = {}
    for s in range(2):
        for f in range(2):
            swaps[s][f].wait_recv()
            sums[f, s] = last[f, s, me.zh] + rc[f, s].astype(F32)
    for ring in first + second:
        ring.drain()
    for swap in swaps[0] + swaps[1]:
        swap.wait_send()
    return [(pl.ds(f * HALF + s * PART, PART), sums[f, s]) for f in range(2) for s in range(2)]


def reduce_scratch():
    dma = pltpu.SemaphoreType.DMA
    bufs = [
        pltpu.VMEM((2, 2, 2, 3, 4, 16, PART), BF16),
        pltpu.VMEM((2, 2, 2, 4, 16, PART), BF16),
        pltpu.VMEM((2, 2, 2, 3, 16, PART), BF16),
        pltpu.VMEM((2, 2, 2, 16, PART), BF16),
        pltpu.VMEM((2, 2, 4, 2, 16, PART), BF16),
        pltpu.VMEM((2, 2, 2, 16, PART), F32),
        pltpu.VMEM((2, 2, 2, 16, PART), BF16),
        pltpu.VMEM((2, 2, 16, PART), BF16),
    ]
    sems = [dma((2, 2, 2, 3))] * 4 + [dma((2, 2))] * 2
    return bufs, sems


class Relay:
    def __init__(self, me, source, stage, parts, sems):
        self.me, self.source, self.stage, self.parts = me, source, stage, parts
        self.s, self.own, self.r, self.zs, self.zr, self.cs, self.cr, self.ps, self.pr = sems

    def hop(self, turn):
        line = turn // 2
        return turn % 2, line + (line // 2) * (5 - 2 * line)

    def holder(self, step):
        me = self.me
        apart, dx = self.hop(step // 4)
        other = ((me.x + dx) % 4) * 8 + ((me.zh + apart) % 2) * 4 + (me.y + step) % 4
        return other, apart, ((me.zl + apart) % 2) * 2 + me.core

    def slot(self, turn):
        apart, dx = self.hop(turn)
        return apart * 4 + (self.me.x + 4 - dx) % 4

    def group(self, slot, flip_z, flip_c):
        me = self.me
        apart = slot // 4
        zl = (me.zl + apart + flip_z) % 2
        core = (me.core + flip_c) % 2
        return (zl * 2 + core) * 8 + (slot % 4) * 2 + (me.zh + apart) % 2

    def at(self, group, part=None, rows=None):
        ref = self.stage
        if len(ref.shape) == 4:
            span = slice(None) if part is None else self.parts[part]
            return ref.at[span, group] if rows is None else ref.at[span, group, rows]
        return ref.at[group] if rows is None else ref.at[group, rows]

    def own_piece(self):
        me = self.me
        mine = me.dp * 8 + me.x * 2 + me.zh
        return self.at(mine, rows=pl.ds(pl.multiple_of(me.y * 32, 32), 32))

    def send(self, batch):
        me = self.me

        def body(step, carry):
            other, apart, group = self.holder(step)
            remote(
                self.source.at[other],
                self.own_piece(),
                self.s.at[batch],
                self.r.at[apart * 4 + me.x],
                (group, other),
            ).start()
            return carry

        if batch == 0:
            pltpu.make_async_copy(self.source.at[me.t], self.own_piece(), self.own).start()
        lax.fori_loop(max(1, 8 * batch), 8 * batch + 8, body, 0)

    def sent(self, batch):
        pieces = self.source.at[pl.ds(0, 7 if batch == 0 else 8)]
        remote(pieces, pieces, self.s.at[batch], self.s.at[batch], (self.me.core_pair, self.me.t)).wait_send()

    def settle(self):
        pltpu.make_async_copy(self.source.at[self.me.t], self.own_piece(), self.own).wait()

    def wait_slot(self, slot):
        me = self.me
        group = self.group(slot, 0, 0)

        def got(count):
            ref = self.at(group, rows=pl.ds(0, count))
            remote(ref, ref, self.s.at[0], self.r.at[slot], (me.core_pair, me.t)).wait_recv()

        @pl.when(slot != me.x)
        def _():
            got(128)

        @pl.when(slot == me.x)
        def _():
            got(96)

    def to_z(self, slot, part=0):
        ref = self.at(self.group(slot, 0, 0), part)
        return remote(ref, ref, self.zs.at[part, slot], self.zr.at[part, slot], (self.me.z_pair, self.me.t))

    def to_core(self, slot):
        ref = self.at(self.group(slot, 0, 0))
        return remote(ref, ref, self.cs.at[slot], self.cr.at[slot], (self.me.core_pair, self.me.t))

    def pass_on(self, slot, part=0):
        ref = self.at(self.group(slot, 1, 0), part)
        return remote(ref, ref, self.ps.at[part, slot], self.pr.at[part, slot], (self.me.core_pair, self.me.t))

    def got(self, ref, sem):
        remote(ref, ref, self.s.at[0], sem, (self.me.core_pair, self.me.t)).wait_recv()

    def each(self, first, last, act):
        def body(turn, carry):
            act(self.slot(turn))
            return carry

        lax.fori_loop(first, last, body, 0)

    def forward(self, first, last):
        def act(slot):
            self.wait_slot(slot)
            self.to_z(slot).start()
            self.to_core(slot).start()

        self.each(first, last, act)

    def relay_on(self, first, last, part=0):
        def act(slot):
            self.got(self.at(self.group(slot, 1, 0), part), self.zr.at[part, slot])
            self.pass_on(slot, part).start()

        self.each(first, last, act)

    def cores(self):
        self.each(0, 8, lambda slot: self.got(self.at(self.group(slot, 0, 1)), self.cr.at[slot]))

    def complete(self, part=0):
        self.each(
            0, 8, lambda slot: self.got(self.at(self.group(slot, 1, 1), part), self.pr.at[part, slot])
        )

    def drain(self):
        def act(slot):
            self.to_core(slot).wait_send()
            for part in range(len(self.parts)):
                self.to_z(slot, part).wait_send()
                self.pass_on(slot, part).wait_send()

        self.each(0, 8, act)


def norm_rows(values, gain):
    center = values - jnp.mean(values, axis=-1, keepdims=True)
    spread = jnp.mean(center * center, axis=-1, keepdims=True)
    return (center * lax.rsqrt(spread + EPSILON) * gain).astype(BF16)


def gather_rows(me, field, view, axes, s_sem, r_sem, pump):
    plan = []
    for f in range(2):
        axis = axes[f]
        p = me.x if axis == "x" else me.y
        for way in range(2):
            delta = 1 - 2 * way
            device = me.near(axis, delta)
            unit = view(f, p, None)
            came = view(f, (p + 4 - delta) % 4, way)
            plan.append(
                (
                    remote(unit, unit, s_sem.at[f, way, 0], r_sem.at[f, way, 0], device),
                    remote(came, came, s_sem.at[f, way, 1], r_sem.at[f, way, 1], device),
                )
            )
    for whole, half in plan:
        whole.start()
    pump(2)
    for whole, half in plan:
        whole.wait_recv()
        half.start()
    pump(1)
    for whole, half in plan:
        half.wait_recv()
    for whole, half in plan:
        whole.wait_send()
        half.wait_send()


def attend(queries, keys, values, seg, slope, context):
    scale = 1.0 / math.sqrt(HD)
    for block in range(4):
        rows = pl.ds(block * 128, 128)
        reach = (block + 1) * 128
        cols = pl.ds(0, reach)
        scores = (
            lax.dot_general(
                queries[rows, :], keys[cols, :], (((1,), (1,)), ((), ())), preferred_element_type=F32
            )
            * scale
        )
        n = lax.broadcasted_iota(jnp.int32, (128, reach), 0) + block * 128
        p = lax.broadcasted_iota(jnp.int32, (128, reach), 1)
        scores = scores - slope * (n - p).astype(F32)
        own = jnp.broadcast_to(seg[:, rows], (128, 128)).T[:, 0:1]
        allowed = (own == seg[:, cols]) & (p <= n)
        scores = jnp.where(allowed, scores, -jnp.inf)
        highest = jnp.max(scores, axis=-1, keepdims=True)
        raised = jnp.exp(scores - highest)
        weights = (raised / jnp.sum(raised, axis=-1, keepdims=True)).astype(BF16)
        context[rows, :] = jnp.dot(weights, values[cols, :], preferred_element_type=F32).astype(BF16)


def layer_kernel(*refs):
    (hidden, seg, slope, gain_one, gain_two, q_in, o_in, u_in, w_in) = refs[:9]
    (result, k_v, v_v, qo, turned, up, normed) = refs[9:16]
    rest = refs[16:]
    (q_f, o_f, u_f, w_f, h_v, sq, su, sw, down, field, share, acc, q_v, ctx, act, middle) = rest[:16]
    in_sem = rest[16]
    relay_sems = [rest[17 + 9 * k : 26 + 9 * k] for k in range(3)]
    rest = rest[44:]
    bufs_one, sems_one, bufs_two, sems_two = rest[:8], rest[8:14], rest[14:22], rest[22:28]
    a_s, a_r, b_s, b_r, x_s, x_r = rest[28:]
    me = Place()

    loads = [
        pltpu.make_async_copy(src, dst, in_sem.at[k])
        for k, (src, dst) in enumerate(
            ((q_in, q_f), (o_in, o_f), (u_in, u_f), (w_in, w_f), (hidden, h_v))
        )
    ]
    loads[0].start()
    loads[1].start()
    r_q = Relay(me, sq, qo, (pl.ds(0, 3), pl.ds(3, 1)), relay_sems[0])
    r_u = Relay(me, su, up, (None,), relay_sems[1])
    r_d = Relay(me, sw, down, (None,), relay_sems[2])

    barrier = pltpu.get_barrier_semaphore()

    def hello(step, carry):
        other, _, group = r_q.holder(step)
        greet(barrier, (group, other))
        return carry

    lax.fori_loop(1, 32, hello, 0)
    greet(barrier, (me.z_pair, me.t))
    greet(barrier, (me.core_pair, me.t))
    greet(barrier, me.across())
    loads[0].wait()
    loads[1].wait()
    for load in loads[2:]:
        load.start()

    @pl.loop(0, 32)
    def _(part):
        cols = pl.ds(pl.multiple_of(part * 128, 128), 128)
        sq[part, 0:3] = q_f[:, :, cols].astype(BF16)
        sq[part, 3] = o_f[:, cols].astype(BF16)

    pl.semaphore_wait(barrier, 34)
    r_q.send(0)

    def cast(source, target):
        @pl.loop(0, 32)
        def _(part):
            cols = pl.ds(pl.multiple_of(part * 512, 512), 512)
            target[part] = source[:, cols].astype(BF16)

    r_q.sent(0)
    r_q.send(1)
    r_q.send(2)
    r_q.settle()
    r_q.forward(0, 2)
    loads[2].wait()
    cast(u_f, su)
    r_q.sent(1)
    r_q.sent(2)
    r_q.send(3)
    r_q.forward(2, 6)
    loads[3].wait()
    cast(w_f, sw)
    r_q.sent(3)
    for batch in range(4):
        r_u.send(batch)
    r_q.forward(6, 8)
    r_q.each(0, 8, lambda slot: r_q.to_z(slot, 1).start())
    loads[4].wait()

    def passing(turn, carry):
        @pl.loop(0, 2)
        def _(part):
            rows = pl.ds(pl.multiple_of(turn * 64 + part * 32, 32), 32)
            normed[rows, :] = norm_rows(h_v[rows, :].astype(F32), gain_one[...])

        r_q.relay_on(turn, turn + 1)
        return carry

    lax.fori_loop(0, 8, passing, 0)
    turns = [(relay, turn) for relay in (r_u, r_d) for turn in range(8)]
    done = [0]

    def pump(count):
        for _ in range(count):
            n = done[0]
            done[0] = n + 1
            if n < 16:
                relay, turn = turns[n]
                slot = relay.slot(turn)
                relay.wait_slot(slot)
                relay.to_z(slot).start()
                relay.to_core(slot).start()
            if n >= 4:
                relay, turn = turns[n - 4]
                relay.relay_on(turn, turn + 1)

    r_u.settle()
    pump(2)
    for batch in range(4):
        r_u.sent(batch)
    for batch in range(4):
        r_d.send(batch)
    r_q.cores()
    r_q.complete()

    acc_q = acc.at[:, pl.ds(0, 384)]
    for part in range(8):
        cols = pl.ds(part * 512, 512)
        block = jnp.concatenate(
            [qo[k, part * 4 : part * 4 + 4].reshape(512, 128) for k in range(3)], axis=1
        )
        product = jnp.dot(normed[:, cols], block, preferred_element_type=F32)
        if part == 0:
            acc_q[...] = product
        else:
            acc_q[...] += product
    pump(1)
    q_v[...] = acc[:, 0:128].astype(BF16)
    k_v[...] = acc[:, 128:256].astype(BF16)
    v_v[...] = acc[:, 256:384].astype(BF16)
    attend(q_v, k_v, v_v, seg, slope[0:1, 0:1], ctx)
    pump(1)
    r_q.relay_on(0, 8, 1)
    r_q.complete(1)
    r_d.settle()

    @pl.loop(0, 8)
    def _(part):
        block = qo[3, pl.ds(part * 4, 4)].reshape(512, 128)
        product = lax.dot_general(
            ctx[...], block, (((1,), (1,)), ((), ())), preferred_element_type=F32
        ).astype(BF16)
        cols = pl.ds(pl.multiple_of(part * 512, 512), 512)
        share[:, :, :, :, cols] = product.reshape(4, 2, 4, 16, 512)

    pump(1)

    def turn_out(first, last):
        @pl.loop(first, last)
        def _(part):
            cols = pl.ds(pl.multiple_of(part * 128, 128), 128)
            turned[:, cols] = qo[3, part].T

    def turn_down(first, last):
        @pl.loop(first, last)
        def _(part):
            cols = pl.ds(pl.multiple_of(part * 128, 128), 128)
            normed[:, cols] = down[part].T

    own_rows = pl.ds(pl.multiple_of(me.t * 16, 16), 16)
    for cols, total in reduce_rows(
        me, share, bufs_one, sems_one, lambda: turn_out(0, 32), lambda: None, pump
    ):
        middle[:, cols] = (h_v[own_rows, cols].astype(F32) + total).astype(BF16)
    field[me.x, me.zh, me.y] = norm_rows(middle[...].astype(F32), gain_two[...])

    spot = field.at[me.x, me.zh, me.y]
    swap = remote(spot, spot, x_s, x_r, me.across())
    swap.start()
    swap.wait_recv()
    swap.wait_send()

    def view_b(f, q, h):
        cols = pl.ds(f * HALF, HALF)
        lane = slice(None) if h is None else h
        if f == 0:
            return field.at[me.x, lane, q, :, cols]
        return field.at[q, lane, me.y, :, cols]

    def view_a(f, q, h):
        cols = pl.ds(f * HALF, HALF)
        lane = slice(None) if h is None else h
        if f == 0:
            return field.at[q, lane, :, :, cols]
        return field.at[:, lane, q, :, cols]

    gather_rows(me, field, view_b, ("y", "x"), b_s, b_r, pump)
    gather_rows(me, field, view_a, ("x", "y"), a_s, a_r, pump)
    pump(20 - done[0])
    r_u.cores()
    r_u.complete()

    for part in range(8):
        rows = field[:, :, :, :, part * 512 : part * 512 + 512].reshape(512, 512)
        block = up[part * 4 : part * 4 + 4].reshape(512, 512)
        product = jnp.dot(rows, block, preferred_element_type=F32)
        if part == 0:
            acc[...] = product
        else:
            acc[...] += product

    @pl.loop(0, 8)
    def _(part):
        rows = pl.ds(pl.multiple_of(part * 64, 64), 64)
        values = acc[rows, :]
        act[rows, :] = (0.5 * values * (1.0 + lax.erf(values * math.sqrt(0.5)))).astype(BF16)

    r_d.cores()
    r_d.complete()

    @pl.loop(0, 8)
    def _(part):
        block = down[pl.ds(part * 4, 4)].reshape(512, 512)
        product = lax.dot_general(
            act[...], block, (((1,), (1,)), ((), ())), preferred_element_type=F32
        ).astype(BF16)
        cols = pl.ds(pl.multiple_of(part * 512, 512), 512)
        share[:, :, :, :, cols] = product.reshape(4, 2, 4, 16, 512)


    for cols, total in reduce_rows(
        me, share, bufs_two, sems_two, lambda: turn_down(0, 16), lambda: turn_down(16, 32)
    ):
        result[:, cols] = (middle[:, cols].astype(F32) + total).astype(BF16)
    for batch in range(4):
        r_d.sent(batch)
    for relay in (r_q, r_u, r_d):
        relay.drain()


def layer(hidden, seg, slope, gain_one, gain_two, qkv, out, up, down):
    any_spec = pl.BlockSpec(memory_space=pl.ANY)
    vmem = pl.BlockSpec(memory_space=pltpu.VMEM)
    dma = pltpu.SemaphoreType.DMA
    bufs_one, sems_one = reduce_scratch()
    bufs_two, sems_two = reduce_scratch()
    def relay_sems(parts):
        one, many = dma((8,)), dma((parts, 8))
        return [dma((4,)), dma(()), one, many, many, one, one, many, many]

    return pl.pallas_call(
        layer_kernel,
        out_shape=(
            pltpu.VMEM((16, D), BF16),
            pltpu.VMEM((512, HD), BF16),
            pltpu.VMEM((512, HD), BF16),
            pltpu.VMEM((4, 32, 128, HD), BF16),
            pltpu.VMEM((HD, D), BF16),
            pltpu.VMEM((32, 128, 512), BF16),
            pltpu.VMEM((512, D), BF16),
        ),
        in_specs=[any_spec, vmem, vmem, vmem, vmem] + [any_spec] * 4,
        out_specs=[vmem] * 7,
        scratch_shapes=[
            pltpu.VMEM((3, 32, 4096), F32),
            pltpu.VMEM((32, 4096), F32),
            pltpu.VMEM((32, 16384), F32),
            pltpu.VMEM((32, 16384), F32),
            pltpu.VMEM((512, D), BF16),
            pltpu.VMEM((32, 4, 32, 128), BF16),
            pltpu.VMEM((32, 32, 512), BF16),
            pltpu.VMEM((32, 32, 512), BF16),
            pltpu.VMEM((32, 128, 512), BF16),
            pltpu.VMEM((4, 2, 4, 16, D), BF16),
            pltpu.VMEM((4, 2, 4, 16, D), BF16),
            pltpu.VMEM((512, 512), F32),
            pltpu.VMEM((512, HD), BF16),
            pltpu.VMEM((512, HD), BF16),
            pltpu.VMEM((512, 512), BF16),
            pltpu.VMEM((16, D), BF16),
            dma((5,)),
        ]
        + relay_sems(2)
        + relay_sems(1)
        + relay_sems(1)
        + bufs_one
        + sems_one
        + bufs_two
        + sems_two
        + [dma((2, 2, 2))] * 4
        + [dma(()), dma(())],
        compiler_params=pltpu.CompilerParams(
            collective_id=0, has_side_effects=True, vmem_limit_bytes=46 << 20
        ),
        name="layer",
    )(hidden, seg.reshape(1, 512), slope, gain_one, gain_two, qkv, out, up, down)


def store_kernel(*refs):
    sem = refs[14]
    copies = [
        pltpu.make_async_copy(refs[k].at[pl.ds(0, refs[7 + k].shape[0])], refs[7 + k], sem.at[k])
        for k in range(7)
    ]
    for copy in copies:
        copy.start()
    for copy in copies:
        copy.wait()


def store(values):
    any_spec = pl.BlockSpec(memory_space=pl.ANY)
    vmem = pl.BlockSpec(memory_space=pltpu.VMEM)
    return pl.pallas_call(
        store_kernel,
        out_shape=[
            jax.ShapeDtypeStruct((3,) + value.shape[1:] if k == 3 else value.shape, value.dtype)
            for k, value in enumerate(values)
        ],
        in_specs=[any_spec] * 7,
        out_specs=[any_spec] * 7,
        scratch_shapes=[pltpu.SemaphoreType.DMA((7,))],
        compiler_params=pltpu.CompilerParams(vmem_limit_bytes=1 << 20),
        name="store",
    )(*values)


def shards(
    hidden, segment_ids, first_gain, second_gain, qkv_master, out_master, up_master, down_master
):
    slope = jnp.exp2(-8.0 * (lax.axis_index("tensor").astype(F32) + 1.0) / (D // HD))
    made = layer(
        hidden,
        segment_ids,
        jnp.full((1, 128), slope, F32),
        first_gain.reshape(1, D),
        second_gain.reshape(1, D),
        qkv_master.transpose(1, 0, 2),
        out_master.T,
        up_master,
        down_master.T,
    )
    new_hidden, keys, values, qkv, out_block, up, down_block = store(made)
    return (
        new_hidden,
        keys,
        values,
        qkv.reshape(3, D, HD).transpose(1, 0, 2),
        out_block,
        up.reshape(D, 512),
        down_block,
    )


def solution(mesh):
    in_specs = (
        P("dp", None),
        P("dp"),
        P(),
        P(),
        P(("dp", "tensor"), None, None),
        P(None, ("dp", "tensor")),
        P(("dp", "tensor"), None),
        P(None, ("dp", "tensor")),
    )
    out_specs = (
        P(("dp", "tensor"), None),
        P("dp", "tensor"),
        P("dp", "tensor"),
        P(None, None, "tensor"),
        P("tensor", None),
        P(None, "tensor"),
        P("tensor", None),
    )
    return jax.shard_map(shards, mesh=mesh, in_specs=in_specs, out_specs=out_specs, check_vma=False)
```

time: 184 us -> 166 us (0.902)
  local copies, waits for them, and re-layouts: 16.5 us -> 0.51 us
  Pallas kernels: 167 us -> 164 us
    reshape x3 -> x0, local copies, waits for them, and re-layouts: 10.3 us -> none  [the longest x1 6.48 us: shards(): down_t.reshape(D, 512)]
    unnamed x15 -> x0, local copies, waits for them, and re-layouts: 5.66 us -> none
    pallas_call x1 -> x2, Pallas kernels: 167 us -> 164 us  [the longest x1 159 us: layer(): pl.pallas_call(layer_kernel, out_shape=(pltpu.VMEM((16, D), BF16), pltpu....]
where the time goes in v3:
time: 166 us; the launch traced here: 165 us
  Pallas kernels  164 us (99%)
    pallas_call x1, Pallas kernels, layer(): pl.pallas_call(layer_kernel, out_shape=(pltpu.VMEM((16, D), BF16), pltpu....  159 us
    pallas_call x1, Pallas kernels, store(): pl.pallas_call(store_kernel, out_shape=[jax.ShapeDtypeStruct((3,) + value...  4.85 us

profile of v3, /device:TPU:0, one launch (start us, length us, event | category | flops | bytes accessed | tf_op | source)
XLA Modules:
  0.0 165.0 jit_solution(17251035419324364624)
XLA Ops:
  0.7 0.5 broadcast_in_dim.3.refs_2_
  1.2 159.0 %layer.1 = (bf16[16,4096]{1,0:T(8,128)(2,1)S(1)}, bf16[512,128]{1,0:T(8,128)(2,1)S(1)}, bf16[512,128]{1,0:T(8,128)(2,1)S(1)}, bf16[4,32,128,128]{3,2,1,0:T(8,128...) custom-call(bf16[512,4096]{1,0:T(8,128)(2,1)} %refs_0_.1, ...), custom_call_target="tpu_custom_call" | custom-call | tf_op jit(solution)/shard_map/layer/pallas_call | solution.py:626
  160.2 4.8 %store.1 = (bf16[16,4096]{1,0:T(8,128)(2,1)}, bf16[512,128]{1,0:T(8,128)(2,1)}, bf16[512,128]{1,0:T(8,128)(2,1)}, bf16[3,32,128,128]{3,2,1,0:T(8,128)(2,1)}, bf1...) custom-call(bf16[16,4096]{1,0:T(8,128)(2,1)S(1)} %get-tuple-element.21.refs_0_, ...), custom_call_target="tpu_custom_call" | custom-call | tf_op jit(solution)/shard_map/store/pallas_call | solution.py:689

commit v4 on v3

--- a/solution.py
+++ b/solution.py
@@ -55,7 +55,7 @@
 PART = 1024
 
 
-def reduce_rows(me, share, bufs, sems, while_first, while_second, pump=lambda count: None):
+def reduce_rows(me, share, bufs, sems, fill, while_first, while_second, pump=lambda count: None):
     ra, acc_a, rb, acc_b, kept, last, last_half, rc = bufs
     sa, qa, sb, qb, sc, qc = sems
     axes = (("x", "y"), ("y", "x"))
@@ -137,10 +137,12 @@
         [remote(last_half.at[f, s, 1 - me.zh], rc.at[f, s], sc.at[f, s], qc.at[f, s], me.across()) for f in range(2)]
         for s in range(2)
     ]
+    fill(0)
     first[0].start(0)
     first[0].start(1)
+    pump(1)
+    fill(1)
     first[1].start(0)
-    pump(1)
     while_first()
     pump(1)
     first[0].accumulate()
@@ -333,34 +335,81 @@
     return (center * lax.rsqrt(spread + EPSILON) * gain).astype(BF16)
 
 
-def gather_rows(me, field, view, axes, s_sem, r_sem, pump):
-    plan = []
-    for f in range(2):
-        axis = axes[f]
-        p = me.x if axis == "x" else me.y
-        for way in range(2):
-            delta = 1 - 2 * way
-            device = me.near(axis, delta)
-            unit = view(f, p, None)
-            came = view(f, (p + 4 - delta) % 4, way)
-            plan.append(
-                (
-                    remote(unit, unit, s_sem.at[f, way, 0], r_sem.at[f, way, 0], device),
-                    remote(came, came, s_sem.at[f, way, 1], r_sem.at[f, way, 1], device),
+def gather_rows(me, field, swap, sems, pump):
+    a_s, a_r, b_s, b_r = sems
+
+    def view_b(f, part, q, half):
+        z = me.zh if part == 0 else 1 - me.zh
+        cols = pl.ds(f * HALF, HALF) if half is None else pl.ds(f * HALF + half * PART, PART)
+        if f == 0:
+            return field.at[me.x, z, q, :, cols]
+        return field.at[q, z, me.y, :, cols]
+
+    def view_a(f, part, q, half):
+        z = me.zh if part == 0 else 1 - me.zh
+        cols = pl.ds(f * HALF, HALF)
+        some = slice(None) if half is None else pl.ds(2 * half, 2)
+        if f == 0:
+            return field.at[q, z, some, :, cols]
+        return field.at[some, z, q, :, cols]
+
+    def ring(part, view, axes, s_sem, r_sem):
+        plan = []
+        for f in range(2):
+            axis = axes[f]
+            p = me.x if axis == "x" else me.y
+            for way in range(2):
+                delta = 1 - 2 * way
+                device = me.near(axis, delta)
+                unit = view(f, part, p, None)
+                came = view(f, part, (p + 4 - delta) % 4, way)
+                at = (part, f, way)
+                plan.append(
+                    (
+                        remote(unit, unit, s_sem.at[at + (0,)], r_sem.at[at + (0,)], device),
+                        remote(came, came, s_sem.at[at + (1,)], r_sem.at[at + (1,)], device),
+                    )
                 )
-            )
-    for whole, half in plan:
-        whole.start()
+        return plan
+
+    def begin(plan):
+        for whole, half in plan:
+            whole.start()
+
+    def turn(plan):
+        for whole, half in plan:
+            whole.wait_recv()
+            half.start()
+
+    def end(plan):
+        for whole, half in plan:
+            half.wait_recv()
+
+    near = [ring(part, view_b, ("y", "x"), b_s, b_r) for part in range(2)]
+    wide = [ring(part, view_a, ("x", "y"), a_s, a_r) for part in range(2)]
+    swap.start()
+    begin(near[0])
+    swap.wait_recv()
+    begin(near[1])
     pump(2)
-    for whole, half in plan:
-        whole.wait_recv()
-        half.start()
-    pump(1)
-    for whole, half in plan:
-        half.wait_recv()
-    for whole, half in plan:
-        whole.wait_send()
-        half.wait_send()
+    turn(near[0])
+    turn(near[1])
+    end(near[0])
+    begin(wide[0])
+    end(near[1])
+    begin(wide[1])
+    pump(2)
+    turn(wide[0])
+    pump(1)
+    turn(wide[1])
+    pump(1)
+    end(wide[0])
+    end(wide[1])
+    for plan in near + wide:
+        for whole, half in plan:
+            whole.wait_send()
+            half.wait_send()
+    swap.wait_send()
 
 
 def attend(queries, keys, values, seg, slope, context):
@@ -388,9 +437,9 @@
 
 
 def layer_kernel(*refs):
-    (hidden, seg, slope, gain_one, gain_two, q_in, o_in, u_in, w_in) = refs[:9]
-    (result, k_v, v_v, qo, turned, up, normed) = refs[9:16]
-    rest = refs[16:]
+    (hidden, seg, gain_one, gain_two, q_in, o_in, u_in, w_in) = refs[:8]
+    (result, k_v, v_v, qo, turned, up, normed) = refs[8:15]
+    rest = refs[15:]
     (q_f, o_f, u_f, w_f, h_v, sq, su, sw, down, field, share, acc, q_v, ctx, act, middle) = rest[:16]
     in_sem = rest[16]
     relay_sems = [rest[17 + 9 * k : 26 + 9 * k] for k in range(3)]
@@ -471,7 +520,11 @@
         r_q.relay_on(turn, turn + 1)
         return carry
 
-    lax.fori_loop(0, 8, passing, 0)
+    lax.fori_loop(0, 4, passing, 0)
+    for batch in range(4):
+        passing(4 + batch, 0)
+        r_u.sent(batch)
+        r_d.send(batch)
     turns = [(relay, turn) for relay in (r_u, r_d) for turn in range(8)]
     done = [0]
 
@@ -491,10 +544,6 @@
 
     r_u.settle()
     pump(2)
-    for batch in range(4):
-        r_u.sent(batch)
-    for batch in range(4):
-        r_d.send(batch)
     r_q.cores()
     r_q.complete()
 
@@ -513,20 +562,37 @@
     q_v[...] = acc[:, 0:128].astype(BF16)
     k_v[...] = acc[:, 128:256].astype(BF16)
     v_v[...] = acc[:, 256:384].astype(BF16)
-    attend(q_v, k_v, v_v, seg, slope[0:1, 0:1], ctx)
+    head = jnp.full((1, 128), me.t + 1, jnp.int32).astype(F32)
+    attend(q_v, k_v, v_v, seg, jnp.exp2(-8.0 * head / (D // HD))[:, 0:1], ctx)
     pump(1)
     r_q.relay_on(0, 8, 1)
     r_q.complete(1)
     r_d.settle()
 
-    @pl.loop(0, 8)
-    def _(part):
-        block = qo[3, pl.ds(part * 4, 4)].reshape(512, 128)
-        product = lax.dot_general(
-            ctx[...], block, (((1,), (1,)), ((), ())), preferred_element_type=F32
-        ).astype(BF16)
-        cols = pl.ds(pl.multiple_of(part * 512, 512), 512)
-        share[:, :, :, :, cols] = product.reshape(4, 2, 4, 16, 512)
+    def columns(i, part):
+        return i % 2 + (i // 2) * 4 + 2 * part
+
+    def share_one(part):
+        @pl.loop(0, 4)
+        def _(i):
+            k = columns(i, part)
+            block = qo[3, pl.ds(k * 4, 4)].reshape(512, 128)
+            product = lax.dot_general(
+                ctx[...], block, (((1,), (1,)), ((), ())), preferred_element_type=F32
+            ).astype(BF16)
+            cols = pl.ds(pl.multiple_of(k * 512, 512), 512)
+            share[:, :, :, :, cols] = product.reshape(4, 2, 4, 16, 512)
+
+    def share_two(part):
+        @pl.loop(0, 4)
+        def _(i):
+            k = columns(i, part)
+            block = down[pl.ds(k * 4, 4)].reshape(512, 512)
+            product = lax.dot_general(
+                act[...], block, (((1,), (1,)), ((), ())), preferred_element_type=F32
+            ).astype(BF16)
+            cols = pl.ds(pl.multiple_of(k * 512, 512), 512)
+            share[:, :, :, :, cols] = product.reshape(4, 2, 4, 16, 512)
 
     pump(1)
 
@@ -544,33 +610,14 @@
 
     own_rows = pl.ds(pl.multiple_of(me.t * 16, 16), 16)
     for cols, total in reduce_rows(
-        me, share, bufs_one, sems_one, lambda: turn_out(0, 32), lambda: None, pump
+        me, share, bufs_one, sems_one, share_one, lambda: turn_out(0, 32), lambda: None, pump
     ):
         middle[:, cols] = (h_v[own_rows, cols].astype(F32) + total).astype(BF16)
     field[me.x, me.zh, me.y] = norm_rows(middle[...].astype(F32), gain_two[...])
 
     spot = field.at[me.x, me.zh, me.y]
     swap = remote(spot, spot, x_s, x_r, me.across())
-    swap.start()
-    swap.wait_recv()
-    swap.wait_send()
-
-    def view_b(f, q, h):
-        cols = pl.ds(f * HALF, HALF)
-        lane = slice(None) if h is None else h
-        if f == 0:
-            return field.at[me.x, lane, q, :, cols]
-        return field.at[q, lane, me.y, :, cols]
-
-    def view_a(f, q, h):
-        cols = pl.ds(f * HALF, HALF)
-        lane = slice(None) if h is None else h
-        if f == 0:
-            return field.at[q, lane, :, :, cols]
-        return field.at[:, lane, q, :, cols]
-
-    gather_rows(me, field, view_b, ("y", "x"), b_s, b_r, pump)
-    gather_rows(me, field, view_a, ("x", "y"), a_s, a_r, pump)
+    gather_rows(me, field, swap, (a_s, a_r, b_s, b_r), pump)
     pump(20 - done[0])
     r_u.cores()
     r_u.complete()
@@ -593,18 +640,8 @@
     r_d.cores()
     r_d.complete()
 
-    @pl.loop(0, 8)
-    def _(part):
-        block = down[pl.ds(part * 4, 4)].reshape(512, 512)
-        product = lax.dot_general(
-            act[...], block, (((1,), (1,)), ((), ())), preferred_element_type=F32
-        ).astype(BF16)
-        cols = pl.ds(pl.multiple_of(part * 512, 512), 512)
-        share[:, :, :, :, cols] = product.reshape(4, 2, 4, 16, 512)
-
-
     for cols, total in reduce_rows(
-        me, share, bufs_two, sems_two, lambda: turn_down(0, 16), lambda: turn_down(16, 32)
+        me, share, bufs_two, sems_two, share_two, lambda: turn_down(0, 16), lambda: turn_down(16, 32)
     ):
         result[:, cols] = (middle[:, cols].astype(F32) + total).astype(BF16)
     for batch in range(4):
@@ -613,7 +650,7 @@
         relay.drain()
 
 
-def layer(hidden, seg, slope, gain_one, gain_two, qkv, out, up, down):
+def layer(hidden, seg, gain_one, gain_two, qkv, out, up, down):
     any_spec = pl.BlockSpec(memory_space=pl.ANY)
     vmem = pl.BlockSpec(memory_space=pltpu.VMEM)
     dma = pltpu.SemaphoreType.DMA
@@ -634,7 +671,7 @@
             pltpu.VMEM((32, 128, 512), BF16),
             pltpu.VMEM((512, D), BF16),
         ),
-        in_specs=[any_spec, vmem, vmem, vmem, vmem] + [any_spec] * 4,
+        in_specs=[any_spec, vmem, vmem, vmem] + [any_spec] * 4,
         out_specs=[vmem] * 7,
         scratch_shapes=[
             pltpu.VMEM((3, 32, 4096), F32),
@@ -662,13 +699,13 @@
         + sems_one
         + bufs_two
         + sems_two
-        + [dma((2, 2, 2))] * 4
+        + [dma((2, 2, 2, 2))] * 4
         + [dma(()), dma(())],
         compiler_params=pltpu.CompilerParams(
             collective_id=0, has_side_effects=True, vmem_limit_bytes=46 << 20
         ),
         name="layer",
-    )(hidden, seg.reshape(1, 512), slope, gain_one, gain_two, qkv, out, up, down)
+    )(hidden, seg.reshape(1, 512), gain_one, gain_two, qkv, out, up, down)
 
 
 def store_kernel(*refs):
@@ -703,11 +740,9 @@
 def shards(
     hidden, segment_ids, first_gain, second_gain, qkv_master, out_master, up_master, down_master
 ):
-    slope = jnp.exp2(-8.0 * (lax.axis_index("tensor").astype(F32) + 1.0) / (D // HD))
     made = layer(
         hidden,
         segment_ids,
-        jnp.full((1, 128), slope, F32),
         first_gain.reshape(1, D),
         second_gain.reshape(1, D),
         qkv_master.transpose(1, 0, 2),

time: 166 us -> 156 us (0.940)
  Pallas kernels: 164 us -> 155 us
    pallas_call x1, Pallas kernels: 159 us -> 151 us  [layer(): pl.pallas_call(layer_kernel, out_shape=(pltpu.VMEM((16, D), BF16), pltpu....]
where the time goes in v4:
time: 156 us
  Pallas kernels  155 us (99%)
    pallas_call x1, Pallas kernels, layer(): pl.pallas_call(layer_kernel, out_shape=(pltpu.VMEM((16, D), BF16), pltpu....  151 us
    pallas_call x1, Pallas kernels, store(): pl.pallas_call(store_kernel, out_shape=[jax.ShapeDtypeStruct((3,) + value...  4.85 us

profile of v4, /device:TPU:0, one launch (start us, length us, event | category | flops | bytes accessed | tf_op | source)
XLA Modules:
  0.0 156.1 jit_solution(709085484817725584)
XLA Ops:
  0.6 150.6 %layer.1 = (bf16[16,4096]{1,0:T(8,128)(2,1)S(1)}, bf16[512,128]{1,0:T(8,128)(2,1)S(1)}, bf16[512,128]{1,0:T(8,128)(2,1)S(1)}, bf16[4,32,128,128]{3,2,1,0:T(8,128...) custom-call(bf16[512,4096]{1,0:T(8,128)(2,1)} %refs_0_.1, ...), custom_call_target="tpu_custom_call" | custom-call | tf_op jit(solution)/shard_map/layer/pallas_call | solution.py:663
  151.3 4.8 %store.1 = (bf16[16,4096]{1,0:T(8,128)(2,1)}, bf16[512,128]{1,0:T(8,128)(2,1)}, bf16[512,128]{1,0:T(8,128)(2,1)}, bf16[3,32,128,128]{3,2,1,0:T(8,128)(2,1)}, bf1...) custom-call(bf16[16,4096]{1,0:T(8,128)(2,1)S(1)} %get-tuple-element.21.refs_0_, ...), custom_call_target="tpu_custom_call" | custom-call | tf_op jit(solution)/shard_map/store/pallas_call | solution.py:726

commit v5 on v4

--- a/solution.py
+++ b/solution.py
@@ -56,7 +56,7 @@
 
 
 def reduce_rows(me, share, bufs, sems, fill, while_first, while_second, pump=lambda count: None):
-    ra, acc_a, rb, acc_b, kept, last, last_half, rc = bufs
+    ra, acc_a, rb, kept, last, last_half, rc = bufs
     sa, qa, sb, qb, sc, qc = sems
     axes = (("x", "y"), ("y", "x"))
 
@@ -66,11 +66,49 @@
             return share.at[q, h, :, :, cols]
         return share.at[:, h, q, :, cols]
 
-    def chunk_b(f, s, q, h):
-        return kept.at[f, s, q, h]
-
     def position(f, level):
         return me.x if axes[f][level] == "x" else me.y
+
+    class Direct:
+        def __init__(self, s):
+            self.s = s
+            self.plan = [
+                (
+                    f,
+                    [
+                        remote(
+                            kept.at[f, s, (position(f, 1) + delta) % 4],
+                            rb.at[f, s, delta - 1],
+                            sb.at[f, s, delta - 1],
+                            qb.at[f, s, delta - 1],
+                            me.near(axes[f][1], delta),
+                        )
+                        for delta in (1, 3, 2)
+                    ],
+                )
+                for f in range(2)
+            ]
+
+        def start(self):
+            for f, copies in self.plan:
+                for copy in copies:
+                    copy.start()
+
+        def finalize(self):
+            s = self.s
+            for f, copies in self.plan:
+                for copy in copies:
+                    copy.wait_recv()
+                total = kept[f, s, position(f, 1)].astype(F32)
+                for k in range(3):
+                    total = total + rb[f, s, k].astype(F32)
+                last[f, s] = total
+                last_half[f, s] = total.astype(BF16)
+
+        def drain(self):
+            for f, copies in self.plan:
+                for copy in copies:
+                    copy.wait_send()
 
     class Ring:
         def __init__(self, level, s, chunk, recv, acc, s_sem, r_sem):
@@ -127,12 +165,8 @@
     def store_a(f, s, h, total):
         kept[f, s, :, h] = total.astype(BF16)
 
-    def store_b(f, s, h, total):
-        last[f, s, h] = total
-        last_half[f, s, h] = total.astype(BF16)
-
     first = [Ring(0, s, chunk_a, ra, acc_a, sa, qa) for s in range(2)]
-    second = [Ring(1, s, chunk_b, rb, acc_b, sb, qb) for s in range(2)]
+    second = [Direct(s) for s in range(2)]
     swaps = [
         [remote(last_half.at[f, s, 1 - me.zh], rc.at[f, s], sc.at[f, s], qc.at[f, s], me.across()) for f in range(2)]
         for s in range(2)
@@ -151,20 +185,16 @@
     first[1].accumulate()
     pump(1)
     first[0].finalize(store_a)
-    second[0].start(0)
-    second[0].start(1)
+    second[0].start()
     pump(1)
     while_second()
-    second[0].accumulate()
     pump(1)
     first[1].finalize(store_a)
-    second[1].start(0)
-    second[1].start(1)
-    second[0].finalize(store_b)
+    second[1].start()
+    second[0].finalize()
     for swap in swaps[0]:
         swap.start()
-    second[1].accumulate()
-    second[1].finalize(store_b)
+    second[1].finalize()
     for swap in swaps[1]:
         swap.start()
     sums = {}
@@ -184,14 +214,13 @@
     bufs = [
         pltpu.VMEM((2, 2, 2, 3, 4, 16, PART), BF16),
         pltpu.VMEM((2, 2, 2, 4, 16, PART), BF16),
-        pltpu.VMEM((2, 2, 2, 3, 16, PART), BF16),
-        pltpu.VMEM((2, 2, 2, 16, PART), BF16),
+        pltpu.VMEM((2, 2, 3, 2, 16, PART), BF16),
         pltpu.VMEM((2, 2, 4, 2, 16, PART), BF16),
         pltpu.VMEM((2, 2, 2, 16, PART), F32),
         pltpu.VMEM((2, 2, 2, 16, PART), BF16),
         pltpu.VMEM((2, 2, 16, PART), BF16),
     ]
-    sems = [dma((2, 2, 2, 3))] * 4 + [dma((2, 2))] * 2
+    sems = [dma((2, 2, 2, 3))] * 2 + [dma((2, 2, 3))] * 2 + [dma((2, 2))] * 2
     return bufs, sems
 
 
@@ -338,12 +367,15 @@
 def gather_rows(me, field, swap, sems, pump):
     a_s, a_r, b_s, b_r = sems
 
-    def view_b(f, part, q, half):
+    def direct(part):
         z = me.zh if part == 0 else 1 - me.zh
-        cols = pl.ds(f * HALF, HALF) if half is None else pl.ds(f * HALF + half * PART, PART)
-        if f == 0:
-            return field.at[me.x, z, q, :, cols]
-        return field.at[q, z, me.y, :, cols]
+        plan = []
+        for f, axis in ((0, "y"), (1, "x")):
+            unit = field.at[me.x, z, me.y, :, pl.ds(f * HALF, HALF)]
+            for delta in (1, 3, 2):
+                at = (part, f, delta - 1)
+                plan.append(remote(unit, unit, b_s.at[at], b_r.at[at], me.near(axis, delta)))
+        return plan
 
     def view_a(f, part, q, half):
         z = me.zh if part == 0 else 1 - me.zh
@@ -385,19 +417,19 @@
         for whole, half in plan:
             half.wait_recv()
 
-    near = [ring(part, view_b, ("y", "x"), b_s, b_r) for part in range(2)]
+    near = [direct(part) for part in range(2)]
     wide = [ring(part, view_a, ("x", "y"), a_s, a_r) for part in range(2)]
     swap.start()
-    begin(near[0])
+    for copy in near[0]:
+        copy.start()
     swap.wait_recv()
-    begin(near[1])
+    for copy in near[1]:
+        copy.start()
     pump(2)
-    turn(near[0])
-    turn(near[1])
-    end(near[0])
-    begin(wide[0])
-    end(near[1])
-    begin(wide[1])
+    for part in range(2):
+        for copy in near[part]:
+            copy.wait_recv()
+        begin(wide[part])
     pump(2)
     turn(wide[0])
     pump(1)
@@ -405,7 +437,9 @@
     pump(1)
     end(wide[0])
     end(wide[1])
-    for plan in near + wide:
+    for copy in near[0] + near[1]:
+        copy.wait_send()
+    for plan in wide:
         for whole, half in plan:
             whole.wait_send()
             half.wait_send()
@@ -444,8 +478,8 @@
     in_sem = rest[16]
     relay_sems = [rest[17 + 9 * k : 26 + 9 * k] for k in range(3)]
     rest = rest[44:]
-    bufs_one, sems_one, bufs_two, sems_two = rest[:8], rest[8:14], rest[14:22], rest[22:28]
-    a_s, a_r, b_s, b_r, x_s, x_r = rest[28:]
+    bufs_one, sems_one, bufs_two, sems_two = rest[:7], rest[7:13], rest[13:20], rest[20:26]
+    a_s, a_r, b_s, b_r, x_s, x_r = rest[26:]
     me = Place()
 
     loads = [
@@ -491,20 +525,17 @@
             cols = pl.ds(pl.multiple_of(part * 512, 512), 512)
             target[part] = source[:, cols].astype(BF16)
 
-    r_q.sent(0)
-    r_q.send(1)
-    r_q.send(2)
+    for batch in range(1, 4):
+        r_q.send(batch)
     r_q.settle()
     r_q.forward(0, 2)
     loads[2].wait()
     cast(u_f, su)
-    r_q.sent(1)
-    r_q.sent(2)
-    r_q.send(3)
     r_q.forward(2, 6)
     loads[3].wait()
     cast(w_f, sw)
-    r_q.sent(3)
+    for batch in range(4):
+        r_q.sent(batch)
     for batch in range(4):
         r_u.send(batch)
     r_q.forward(6, 8)
@@ -548,10 +579,10 @@
     r_q.complete()
 
     acc_q = acc.at[:, pl.ds(0, 384)]
-    for part in range(8):
-        cols = pl.ds(part * 512, 512)
+    for part in range(4):
+        cols = pl.ds(part * 1024, 1024)
         block = jnp.concatenate(
-            [qo[k, part * 4 : part * 4 + 4].reshape(512, 128) for k in range(3)], axis=1
+            [qo[k, part * 8 : part * 8 + 8].reshape(1024, 128) for k in range(3)], axis=1
         )
         product = jnp.dot(normed[:, cols], block, preferred_element_type=F32)
         if part == 0:
@@ -622,9 +653,9 @@
     r_u.cores()
     r_u.complete()
 
-    for part in range(8):
-        rows = field[:, :, :, :, part * 512 : part * 512 + 512].reshape(512, 512)
-        block = up[part * 4 : part * 4 + 4].reshape(512, 512)
+    for part in range(4):
+        rows = field[:, :, :, :, part * 1024 : part * 1024 + 1024].reshape(512, 1024)
+        block = up[part * 8 : part * 8 + 8].reshape(1024, 512)
         product = jnp.dot(rows, block, preferred_element_type=F32)
         if part == 0:
             acc[...] = product
@@ -699,7 +730,8 @@
         + sems_one
         + bufs_two
         + sems_two
-        + [dma((2, 2, 2, 2))] * 4
+        + [dma((2, 2, 2, 2))] * 2
+        + [dma((2, 2, 3))] * 2
         + [dma(()), dma(())],
         compiler_params=pltpu.CompilerParams(
             collective_id=0, has_side_effects=True, vmem_limit_bytes=46 << 20

time: 156 us -> 152 us (0.974)
  Pallas kernels: 155 us -> 151 us
    pallas_call x1, Pallas kernels: 151 us -> 146 us  [layer(): pl.pallas_call(layer_kernel, out_shape=(pltpu.VMEM((16, D), BF16), pltpu....]
where the time goes in v5:
time: 152 us; the launch traced here: 151 us
  Pallas kernels  151 us (99%)
    pallas_call x1, Pallas kernels, layer(): pl.pallas_call(layer_kernel, out_shape=(pltpu.VMEM((16, D), BF16), pltpu....  146 us
    pallas_call x1, Pallas kernels, store(): pl.pallas_call(store_kernel, out_shape=[jax.ShapeDtypeStruct((3,) + value...  4.85 us

profile of v5, /device:TPU:0, one launch (start us, length us, event | category | flops | bytes accessed | tf_op | source)
XLA Modules:
  0.0 151.3 jit_solution(13727810637884908146)
XLA Ops:
  0.6 145.8 %layer.1 = (bf16[16,4096]{1,0:T(8,128)(2,1)S(1)}, bf16[512,128]{1,0:T(8,128)(2,1)S(1)}, bf16[512,128]{1,0:T(8,128)(2,1)S(1)}, bf16[4,32,128,128]{3,2,1,0:T(8,128...) custom-call(bf16[512,4096]{1,0:T(8,128)(2,1)} %refs_0_.1, ...), custom_call_target="tpu_custom_call" | custom-call | tf_op jit(solution)/shard_map/layer/pallas_call | solution.py:694
  146.5 4.8 %store.1 = (bf16[16,4096]{1,0:T(8,128)(2,1)}, bf16[512,128]{1,0:T(8,128)(2,1)}, bf16[512,128]{1,0:T(8,128)(2,1)}, bf16[3,32,128,128]{3,2,1,0:T(8,128)(2,1)}, bf1...) custom-call(bf16[16,4096]{1,0:T(8,128)(2,1)S(1)} %get-tuple-element.21.refs_0_, ...), custom_call_target="tpu_custom_call" | custom-call | tf_op jit(solution)/shard_map/store/pallas_call | solution.py:758

commit v6 on v5

--- a/solution.py
+++ b/solution.py
@@ -188,7 +188,6 @@
     second[0].start()
     pump(1)
     while_second()
-    pump(1)
     first[1].finalize(store_a)
     second[1].start()
     second[0].finalize()
@@ -364,7 +363,7 @@
     return (center * lax.rsqrt(spread + EPSILON) * gain).astype(BF16)
 
 
-def gather_rows(me, field, swap, sems, pump):
+def gather_rows(me, field, swap, sems, pump, with_own):
     a_s, a_r, b_s, b_r = sems
 
     def direct(part):
@@ -430,12 +429,13 @@
         for copy in near[part]:
             copy.wait_recv()
         begin(wide[part])
-    pump(2)
+    pump(3)
     turn(wide[0])
     pump(1)
     turn(wide[1])
     pump(1)
     end(wide[0])
+    with_own()
     end(wide[1])
     for copy in near[0] + near[1]:
         copy.wait_send()
@@ -527,18 +527,16 @@
 
     for batch in range(1, 4):
         r_q.send(batch)
-    r_q.settle()
-    r_q.forward(0, 2)
     loads[2].wait()
     cast(u_f, su)
-    r_q.forward(2, 6)
     loads[3].wait()
     cast(w_f, sw)
+    r_q.settle()
+    r_q.forward(0, 8)
     for batch in range(4):
         r_q.sent(batch)
     for batch in range(4):
         r_u.send(batch)
-    r_q.forward(6, 8)
     r_q.each(0, 8, lambda slot: r_q.to_z(slot, 1).start())
     loads[4].wait()
 
@@ -623,7 +621,8 @@
                 act[...], block, (((1,), (1,)), ((), ())), preferred_element_type=F32
             ).astype(BF16)
             cols = pl.ds(pl.multiple_of(k * 512, 512), 512)
-            share[:, :, :, :, cols] = product.reshape(4, 2, 4, 16, 512)
+            share[:, me.zh, :, :, cols] = product[:256].reshape(4, 4, 16, 512)
+            share[:, 1 - me.zh, :, :, cols] = product[256:].reshape(4, 4, 16, 512)
 
     pump(1)
 
@@ -648,26 +647,32 @@
 
     spot = field.at[me.x, me.zh, me.y]
     swap = remote(spot, spot, x_s, x_r, me.across())
-    gather_rows(me, field, swap, (a_s, a_r, b_s, b_r), pump)
+    def hidden_units(part):
+        z = me.zh if part == 0 else 1 - me.zh
+        half = acc.at[pl.ds(part * 256, 256)]
+        for k in range(4):
+            rows = field[:, z, :, :, k * 1024 : k * 1024 + 1024].reshape(256, 1024)
+            block = up[k * 8 : k * 8 + 8].reshape(1024, 512)
+            product = jnp.dot(rows, block, preferred_element_type=F32)
+            if k == 0:
+                half[...] = product
+            else:
+                half[...] += product
+
+        @pl.loop(0, 4)
+        def _(step):
+            rows = pl.ds(pl.multiple_of(part * 256 + step * 64, 64), 64)
+            values = acc[rows, :]
+            act[rows, :] = (0.5 * values * (1.0 + lax.erf(values * math.sqrt(0.5)))).astype(BF16)
+
+    def with_own():
+        r_u.cores()
+        r_u.complete()
+        hidden_units(0)
+
+    gather_rows(me, field, swap, (a_s, a_r, b_s, b_r), pump, with_own)
     pump(20 - done[0])
-    r_u.cores()
-    r_u.complete()
-
-    for part in range(4):
-        rows = field[:, :, :, :, part * 1024 : part * 1024 + 1024].reshape(512, 1024)
-        block = up[part * 8 : part * 8 + 8].reshape(1024, 512)
-        product = jnp.dot(rows, block, preferred_element_type=F32)
-        if part == 0:
-            acc[...] = product
-        else:
-            acc[...] += product
-
-    @pl.loop(0, 8)
-    def _(part):
-        rows = pl.ds(pl.multiple_of(part * 64, 64), 64)
-        values = acc[rows, :]
-        act[rows, :] = (0.5 * values * (1.0 + lax.erf(values * math.sqrt(0.5)))).astype(BF16)
-
+    hidden_units(1)
     r_d.cores()
     r_d.complete()
 

time: 152 us -> 152 us (level)
  no operation moved by 1% of the time
where the time goes in v6:
time: 152 us
  Pallas kernels  151 us (99%)
    pallas_call x1, Pallas kernels, layer(): pl.pallas_call(layer_kernel, out_shape=(pltpu.VMEM((16, D), BF16), pltpu....  146 us
    pallas_call x1, Pallas kernels, store(): pl.pallas_call(store_kernel, out_shape=[jax.ShapeDtypeStruct((3,) + value...  4.85 us

profile of v6, /device:TPU:0, one launch (start us, length us, event | category | flops | bytes accessed | tf_op | source)
XLA Modules:
  0.0 151.6 jit_solution(958758512891219565)
XLA Ops:
  0.6 146.1 %layer.1 = (bf16[16,4096]{1,0:T(8,128)(2,1)S(1)}, bf16[512,128]{1,0:T(8,128)(2,1)S(1)}, bf16[512,128]{1,0:T(8,128)(2,1)S(1)}, bf16[4,32,128,128]{3,2,1,0:T(8,128...) custom-call(bf16[512,4096]{1,0:T(8,128)(2,1)} %refs_0_.1, ...), custom_call_target="tpu_custom_call" | custom-call | tf_op jit(solution)/shard_map/layer/pallas_call | solution.py:699
  146.7 4.8 %store.1 = (bf16[16,4096]{1,0:T(8,128)(2,1)}, bf16[512,128]{1,0:T(8,128)(2,1)}, bf16[512,128]{1,0:T(8,128)(2,1)}, bf16[3,32,128,128]{3,2,1,0:T(8,128)(2,1)}, bf1...) custom-call(bf16[16,4096]{1,0:T(8,128)(2,1)S(1)} %get-tuple-element.21.refs_0_, ...), custom_call_target="tpu_custom_call" | custom-call | tf_op jit(solution)/shard_map/store/pallas_call | solution.py:763
